TPU v7x, 256 devices: a whole 4x4x8 slice. The times are simulated.
256 devices in a mesh: ctx: 16 (over z, y_hi), grp: 16 (over y_lo, x, core).
Axes of the slice: x: 4, y: 4 (y_hi: 2, y_lo: 2; y = y_hi * 2 + y_lo), z: 8, core: 2. Of those that a mesh axis runs over, the one named last changes fastest.
Arguments:
- q_latent: bfloat16 [4096, 1536], P('ctx'), may hold values from -210 to 210
- kv_latent: bfloat16 [4096, 576], P('ctx'), may hold values from -6 to 6
- kv_gain: float32 [512], replicated, may hold values from 0.1 to 1.9
- q_weight: bfloat16 [1536, 24576], P('ctx', 'grp'), may hold values from -0.15625 to 0.15625
- kv_weight: bfloat16 [512, 32768], P('ctx', 'grp'), may hold values from -0.25 to 0.25
- out_weight: bfloat16 [16384, 7168], P('grp', 'ctx'), may hold values from -0.0625 to 0.0625
- documents: int32 [4096], replicated, may hold values from 0 to 7, never falling along the last dimension, each value on 1 to 1024 neighbouring positions
Outputs:
- mixed: bfloat16 [4096, 7168], P('ctx', 'grp')
All inputs are finite; a program needn't handle non-finite values.
Results may differ from a plain program's by a relative error of at most 0.018.
Values may be sent and summed in bfloat16 or wider, within the bound.
A program may use at most 64 MiB of HBM per device.

v0:
```python
import jax
import jax.numpy as jnp
from jax import lax
from jax.sharding import Mesh
from jax.sharding import PartitionSpec as P

KL = 512
NOPE = 128
ROPE = 64
VDIM = 128
CTX = ("ctx_0", "ctx_1")


epsilon = 1e-06


def gather_axes(array, axes, dim):
    result = array
    for number in range(len(axes) - 1, -1, -1):
        result = lax.all_gather(result, axes[number], axis=dim, tiled=True)
    return result


def shifted(block, axis, distance):
    devices = range(lax.axis_size(axis))
    route = [(i - distance, i) for i in devices if i - distance in devices]
    return lax.ppermute(block, axis, route)


def joined_along(tiles, dim):
    lengths = list(tiles.shape[1:])
    lengths[dim] *= tiles.shape[0]
    return jnp.moveaxis(tiles, 0, dim).reshape(lengths)


def copy_for_each(array, axis):
    count = lax.axis_size(axis)
    return lax.all_to_all(
        jnp.broadcast_to(array[None], (count, *array.shape)), axis, 0, 0, tiled=True
    )


def gathered_copies(array, axis, dim):
    return joined_along(copy_for_each(array, axis), dim)


def in_blocks(array, dim, count):
    lengths = array.shape
    tiles = array.reshape(*lengths[:dim], count, lengths[dim] // count, *lengths[dim + 1 :])
    return jnp.moveaxis(tiles, dim, 0)


def summed_on_arrival(array, axis, dim):
    count = lax.axis_size(axis)
    tiles = lax.all_to_all(in_blocks(array, dim, count), axis, 0, 0, tiled=True)
    return jnp.sum(tiles.astype(jnp.float32), axis=0)


def rotate(inputs, positions):
    half_width = inputs.shape[-1] // 2
    inverse = 10000.0 ** (-2.0 * jnp.arange(half_width, dtype=jnp.float32) / inputs.shape[-1])
    angles = positions.astype(jnp.float32)[:, None] * inverse[None, :]
    shape = (angles.shape[0],) + (1,) * (inputs.ndim - 2) + (half_width,)
    cosine = jnp.cos(angles).reshape(shape)
    sine_part = jnp.sin(angles).reshape(shape)
    front_half = inputs[..., :half_width]
    back_half = inputs[..., half_width:]
    return jnp.concatenate(
        [front_half * cosine - back_half * sine_part, back_half * cosine + front_half * sine_part],
        axis=-1,
    )


def prepare(latent_block, positions, kv_gain):
    latent = latent_block[:, :KL].astype(jnp.float32)
    normed = (
        latent * lax.rsqrt(jnp.mean(latent * latent, axis=-1, keepdims=True) + epsilon) * kv_gain
    )
    key_rope = rotate(latent_block[:, KL:].astype(jnp.float32), positions).astype(jnp.bfloat16)
    return (normed.astype(jnp.bfloat16), key_rope)


def folder(left, weight_piece):
    return jnp.dot(left, weight_piece, preferred_element_type=jnp.float32)


def per_device(q_latent, kv_latent, kv_gain, q_weight, kv_weight, out_weight, documents):
    rows_dev = q_latent.shape[0]
    head_count = q_weight.shape[1] // (NOPE + ROPE)
    block_index = lax.axis_index(CTX)
    query_pos = block_index * rows_dev + jnp.arange(rows_dev, dtype=jnp.int32)
    prior_pos = query_pos - rows_dev
    query_full = folder(q_latent, gather_axes(q_weight, CTX, 0))
    query_full = query_full.reshape(rows_dev, head_count, NOPE + ROPE)
    query_nope = query_full[..., :NOPE].astype(jnp.bfloat16)
    query_rope = rotate(query_full[..., NOPE:], query_pos).astype(jnp.bfloat16)
    previous = shifted(kv_latent, CTX, 1)
    latent_block = jnp.concatenate([previous, kv_latent], axis=0)
    positions = jnp.concatenate([prior_pos, query_pos])
    normed, key_rope = prepare(latent_block, positions, kv_gain)
    key_value = folder(normed, gathered_copies(kv_weight, CTX, 0))
    key_value = key_value.astype(jnp.bfloat16)
    key_value = key_value.reshape(2 * rows_dev, head_count, NOPE + VDIM)
    key_nope = key_value[..., :NOPE]
    values = key_value[..., NOPE:]
    key_pos = jnp.concatenate([prior_pos, query_pos])
    query_docs = lax.dynamic_slice_in_dim(documents, block_index * rows_dev, rows_dev, 0)
    prior_docs = lax.dynamic_slice_in_dim(
        documents, jnp.maximum(block_index - 1, 0) * rows_dev, rows_dev, 0
    )
    key_docs = jnp.concatenate([prior_docs, query_docs])
    allowed = (
        (key_docs[None, :] == query_docs[:, None])
        & (key_pos[None, :] <= query_pos[:, None])
        & (key_pos[None, :] >= 0)
    )
    scale = (NOPE + ROPE) ** (-0.5)
    scores = jnp.einsum("qhd,khd->hqk", query_nope, key_nope, preferred_element_type=jnp.float32)
    scores = (
        scores + jnp.einsum("qhr,kr->hqk", query_rope, key_rope, preferred_element_type=jnp.float32)
    ) * scale
    scores = jnp.where(allowed[None], scores, -1e30)
    highest = jnp.max(scores, axis=-1, keepdims=True)
    weights = jnp.exp(scores - highest)
    probs = (weights / jnp.sum(weights, axis=-1, keepdims=True)).astype(jnp.bfloat16)
    attended = jnp.einsum("hqk,khv->qhv", probs, values, preferred_element_type=jnp.float32).astype(
        jnp.bfloat16
    )
    attended = attended.reshape(rows_dev, head_count * VDIM)
    partial_value = jnp.dot(
        attended,
        lax.all_gather(out_weight, CTX, axis=1, tiled=True),
        preferred_element_type=jnp.float32,
    )
    mixed = summed_on_arrival(partial_value.astype(jnp.bfloat16), "grp", 1).astype(jnp.bfloat16)
    return mixed


def solution(mesh):
    torus = Mesh(mesh.devices.reshape(8, 2, mesh.shape["grp"]), ("ctx_0", "ctx_1", "grp"))
    return jax.shard_map(
        per_device,
        mesh=torus,
        in_specs=(
            P(CTX, None),
            P(CTX, None),
            P(),
            P(CTX, "grp"),
            P(CTX, "grp"),
            P("grp", CTX),
            P(),
        ),
        out_specs=P(CTX, "grp"),
        check_vma=False,
    )
```

profile of v0, /device:TPU:8, one launch (start us, length us, event | category | flops | bytes accessed | tf_op | source)
XLA Modules:
  0.0 414.7 jit_solution(16607223282581625902)
XLA Ops:
  6.5 0.0 copy-start
  6.5 0.0 copy-start.3
  6.5 0.0 all-gather.3.cloned.1.call-start
  6.5 12.0 %all_gather.9 = bf16[192,1536]{1,0:T(8,128)(2,1)} all-gather(bf16[96,1536]{1,0:T(8,128)(2,1)} %param.10), channel_id=1, replica_groups=mesh['ctx_0'=8,'ctx_1'=2,'grp'=16] {'ctx_1'}, dimensions={0}, use_global_device_ids=true | all-gather | bytes 884736 | tf_op jit(solution)/shard_map/all_gather | solution.py:20
  18.6 0.0 all-gather.3.cloned.1.call-update
  18.6 0.0 all-gather.5.cloned.1.call-start
  18.6 0.7 all-gather.5.cloned.1.call-update
  19.3 0.0 copy-start.6
  19.4 2.5 broadcast_in_dim.10
  21.9 9.6 %all-to-all-start = ((bf16[16,32,2048]{2,1,0:T(8,128)(2,1)}), bf16[16,32,2048]{2,1,0:T(8,128)(2,1)S(1)}, u32[]{:S(2)}, u32[]{:S(2)}) async-start(bf16[16,32,2048]{2,1,0:T(8,128)(2,1)} %broadcast_in_dim.10), calls=%async_computation | async-start | bytes 4194304 | tf_op jit(solution)/shard_map/all_to_all | solution.py:38
  31.5 0.0 copy-done.3
  31.5 6.1 %collective-permute-start = (bf16[256,576]{0,1:T(8,128)(2,1)S(1)}, bf16[256,576]{0,1:T(8,128)(2,1)}, u32[]{:S(2)}, u32[]{:S(2)}) collective-permute-start(bf16[256,576]{0,1:T(8,128)(2,1)S(1)} %copy-done.3), channel_id=1, source_target_pairs={{0,16},{16,32},{32,48},{48,64},{64,80},{80,96},{96,112},{112,128},... | collective-permute-start | bytes 884744 | tf_op jit(solution)/shard_map/ppermute | solution.py:27
  37.6 0.8 fusion.34
  38.5 0.8 multiply_cosine_fusion.1
  39.3 0.8 and_and_fusion
  40.2 1.5 collective-permute-done
  41.7 1.0 constant_dynamic-update-slice_fusion.1
  42.7 1.0 constant_dynamic-update-slice_fusion
  43.6 0.2 fusion.5
  43.8 0.3 fusion.23
  44.2 59.1 %all-to-all-done = bf16[16,32,2048]{2,1,0:T(8,128)(2,1)S(1)} async-done(((bf16[16,32,2048]{2,1,0:T(8,128)(2,1)}), bf16[16,32,2048]{2,1,0:T(8,128)(2,1)S(1)}, u32[]{:S(2)}, u32[]{:S(2)}) %all-to-all-start) | async-done | bytes 2097184 | tf_op jit(solution)/shard_map/all_to_all | solution.py:38
  103.3 0.0 copy-done.6
  103.3 1.4 convolution_convert_fusion.1
  104.7 0.7 copy.31
  105.4 0.1 fusion.33
  105.5 0.0 copy-start.4
  105.5 0.0 copy-start.5
  105.5 18.4 %all-gather.3.cloned.1.call-done = bf16[1536,1536]{1,0:T(8,128)(2,1)} async-done(((bf16[192,1536]{1,0:T(8,128)(2,1)}), bf16[1536,1536]{1,0:T(8,128)(2,1)}) %all-gather.3.cloned.1.call-update) | async-done | bytes 4718608 | tf_op jit(solution)/shard_map/all_gather | solution.py:20
  123.9 0.0 copy-done
  123.9 4.3 %fusion.36 = f32[256,1536]{0,1:T(8,128)S(1)} fusion(bf16[256,1536]{1,0:T(8,128)(2,1)S(1)} %copy-done, bf16[1536,1536]{1,0:T(8,128)(2,1)} %all-gather.3.cloned.1.call-done), kind=kOutput, calls=%fused_computation.60 | convolution fusion | flops 1207959552 | bytes 7077888 | tf_op jit(solution)/shard_map/dot_general | solution.py:84
  128.2 0.0 copy-start.2
  128.2 0.0 copy-done.4
  128.2 0.0 copy-done.5
  128.2 0.1 subtract_convert_fusion
  128.3 0.8 fusion.8
  129.1 0.0 copy-done.2
  129.1 1.0 fusion.2
  130.1 0.0 copy-start.1
  130.1 2.0 copy-done.1
  132.1 1.7 fusion.35
  133.8 7.5 %fusion.4 = bf16[8,128,256]{2,1,0:T(8,128)(2,1)S(1)} fusion(f32[8,256]{1,0:T(8,128)S(1)} %fusion.35, bf16[512,8,128]{2,1,0:T(8,128)(2,1)S(1)} %get-tuple-element.5, f32[8,256,512]{2,1,0:T(8,128)} %copy-done.1), kind=kOutput, calls=%fused_computation.11 | convolution fusion | flops 271845888 | bytes 5775360 | tf_op jit(solution)/shard_map/hqk,khv->qhv/dot_general | solution.py:126
  141.4 191.9 %all-gather.5.cloned.1.call-done = bf16[1024,7168]{0,1:T(8,128)(2,1)} async-done(((bf16[1024,448]{0,1:T(8,128)(2,1)}), bf16[1024,7168]{0,1:T(8,128)(2,1)}) %all-gather.5.cloned.1.call-update) | async-done | bytes 14680080 | tf_op jit(solution)/shard_map/all_gather | solution.py:132
  333.2 16.4 %convolution_convert_fusion = bf16[256,7168]{1,0:T(8,128)(2,1)} fusion(bf16[256,1024]{0,1:T(8,128)(2,1)S(1)} %bitcast.32, bf16[1024,7168]{0,1:T(8,128)(2,1)} %all-gather.5.cloned.1.call-done), kind=kOutput, calls=%fused_computation.1 | convolution fusion | flops 3759931392 | bytes 18874368 | tf_op jit(solution)/shard_map/dot_general | solution.py:130
  349.6 5.9 %copy.25 = bf16[256,7168]{0,1:T(8,128)(2,1)} copy(bf16[256,7168]{1,0:T(8,128)(2,1)} %convolution_convert_fusion) | data formatting | bytes 7340032 | tf_op jit(solution)/shard_map/convert_element_type | solution.py:135
  355.5 49.0 %all_to_all.10 = bf16[16,256,448]{1,2,0:T(8,128)(2,1)} all-to-all(bf16[16,256,448]{1,2,0:T(8,128)(2,1)} %bitcast.26), channel_id=1, replica_groups=mesh['ctx_0'=8,'ctx_1'=2,'grp'=16] {'grp'}, dimensions={0} | all-to-all | bytes 7340032 | tf_op jit(solution)/shard_map/all_to_all | solution.py:55
  404.5 3.3 reduce_sum.32
  (8 shorter events, 0.1 us)
Async XLA Ops:
  6.5 117.4 %copy-start = (bf16[256,1536]{1,0:T(8,128)(2,1)S(1)}, bf16[256,1536]{1,0:T(8,128)(2,1)}, u32[]{:S(2)}) copy-start(bf16[256,1536]{1,0:T(8,128)(2,1)} %param.7) | copy-start | bytes 2359300
  6.5 25.0 %copy-start.3 = (bf16[256,576]{0,1:T(8,128)(2,1)S(1)}, bf16[256,576]{0,1:T(8,128)(2,1)}, u32[]{:S(2)}) copy-start(bf16[256,576]{0,1:T(8,128)(2,1)} %param.8) | copy-start | bytes 884740
  6.5 117.4 %all-gather.3.cloned.1.call-start = ((), (), s32[]{:S(2)}) async-start(), calls=%async_computation.2 | async-start | bytes 5308416 | tf_op jit(solution)/shard_map/all_gather | solution.py:20
  18.6 314.6 %all-gather.5.cloned.1.call-start = ((), (), s32[]{:S(2)}) async-start(), calls=%async_computation.3 | async-start | bytes 15597568 | tf_op jit(solution)/shard_map/all_gather | solution.py:132
  19.3 83.9 %copy-start.6 = (f32[512]{0:T(512)S(1)}, f32[512]{0:T(512)}, u32[]{:S(2)}) copy-start(f32[512]{0:T(512)} %param.9) | copy-start | bytes 6148
  21.9 81.4 %all-to-all-start = ((bf16[16,32,2048]{2,1,0:T(8,128)(2,1)}), bf16[16,32,2048]{2,1,0:T(8,128)(2,1)S(1)}, u32[]{:S(2)}, u32[]{:S(2)}) async-start(bf16[16,32,2048]{2,1,0:T(8,128)(2,1)} %broadcast_in_dim.10), calls=%async_computation | async-start | bytes 4194304 | tf_op jit(solution)/shard_map/all_to_all | solution.py:38
  31.5 10.2 %collective-permute-start = (bf16[256,576]{0,1:T(8,128)(2,1)S(1)}, bf16[256,576]{0,1:T(8,128)(2,1)}, u32[]{:S(2)}, u32[]{:S(2)}) collective-permute-start(bf16[256,576]{0,1:T(8,128)(2,1)S(1)} %copy-done.3), channel_id=1, source_target_pairs={{0,16},{16,32},{32,48},{48,64},{64,80},{80,96},{96,112},{112,128},... | collective-permute-start | bytes 884744 | tf_op jit(solution)/shard_map/ppermute | solution.py:27
  105.5 22.7 %copy-start.4 = (f32[256,32]{0,1:T(8,128)S(1)}, f32[256,32]{0,1:T(8,128)}, u32[]{:S(2)}) copy-start(f32[256,32]{0,1:T(8,128)} %get-tuple-element.15) | copy-start | bytes 98308
  105.5 22.7 %copy-start.5 = (f32[256,32]{0,1:T(8,128)S(1)}, f32[256,32]{0,1:T(8,128)}, u32[]{:S(2)}) copy-start(f32[256,32]{0,1:T(8,128)} %get-tuple-element.16) | copy-start | bytes 98308
  128.2 0.9 copy-start.2
  130.1 2.0 copy-start.1
Sparse Core Ops, SparseCore 0:
  18.7 105.1 all-gather.2
  126.5 206.6 all-gather.4
where the time goes:
time: 417 us; the launch traced here: 415 us
  waiting for transfers between devices  272 us (65%)
  blocking collectives  61.1 us (15%)
  matrix products  31.3 us (8%)
  starting transfers between devices  15.8 us (4%)
  local copies, waits for them, and re-layouts  14.1 us (3%)
  between operations  13.6 us (3%)
  other arithmetic  7.32 us (2%)
    all_gather x1, waiting for transfers between devices, per_device(): lax.all_gather(out_weight, CTX, axis=1, tiled=True)  192 us
    all_to_all x1, waiting for transfers between devices, copy_for_each(): lax.all_to_all(jnp.broadcast_to(array[None], (count, *array.shape)), axis...  59.1 us
    all_to_all x1, blocking collectives, summed_on_arrival(): tiles = lax.all_to_all(in_blocks(array, dim, count), axis, 0, 0, tiled=True)  49 us
    all_gather x1, waiting for transfers between devices, gather_axes(): result = lax.all_gather(result, axes[number], axis=dim, tiled=True)  18.4 us
    dot_general x1, matrix products, per_device(): jnp.dot(attended, lax.all_gather(out_weight, CTX, axis=1, tiled=True), pr...  16.4 us
    all_gather x1, blocking collectives, gather_axes(): result = lax.all_gather(result, axes[number], axis=dim, tiled=True)  12 us
    all_to_all x1, starting transfers between devices, copy_for_each(): lax.all_to_all(jnp.broadcast_to(array[None], (count, *array.shape)), axis...  9.64 us
  transfers between devices with their start and end apart: 4, of which 4 were waited for; matrix products, arithmetic and copies ran while one was open for 6% of the time, Pallas kernels for 0%

commit v1 on v0

v1 whole, which is shorter than its diff:
```python
import jax
import jax.numpy as jnp
from jax import lax
from jax.experimental import pallas as pl
from jax.experimental.pallas import tpu as pltpu
from jax.sharding import PartitionSpec as P

KL = 512
NOPE = 128
ROPE = 64
VDIM = 128
HEAD = NOPE + ROPE
Z = 8
MESH = pl.DeviceIdType.MESH
ANY = pl.BlockSpec(memory_space=pl.ANY)
VM = pl.BlockSpec(memory_space=pltpu.VMEM)
EPSILON = 1e-06


class Place:
    def __init__(self):
        ctx = lax.axis_index("ctx")
        grp = lax.axis_index("grp")
        self.ctx = ctx
        self.z = ctx // 2
        self.y = ctx % 2
        self.chip = grp // 2
        self.core = grp % 2

    def at(self, z=None, y=None, chip=None, core=None):
        z = self.z if z is None else z
        y = self.y if y is None else y
        chip = self.chip if chip is None else chip
        core = self.core if core is None else core
        return (z * 2 + y, chip * 2 + core)


class Sends:
    def __init__(self, send_sems, recv_sems):
        self.send_sems = send_sems
        self.recv_sems = recv_sems
        self.used = 0
        self.started = []

    def slot(self):
        self.used += 1
        return self.used - 1

    def make(self, number, source, target, device):
        return pltpu.make_async_remote_copy(
            source,
            target,
            self.send_sems.at[number],
            self.recv_sems.at[number],
            device_id=device,
            device_id_type=MESH,
        )

    def start(self, number, source, target, device):
        copy = self.make(number, source, target, device)
        copy.start()
        self.started.append(copy)

    def arrived(self, number, target, device):
        self.make(number, target, target, device).wait_recv()

    def drain(self):
        for copy in self.started:
            copy.wait_send()


def enter(devices):
    barrier = pltpu.get_barrier_semaphore()
    for device in devices:
        pl.semaphore_signal(barrier, inc=1, device_id=device, device_id_type=MESH)
    pl.semaphore_wait(barrier, len(devices))


class Ring:
    def __init__(self, sends, place, views):
        self.sends = sends
        self.place = place
        self.views = views
        self.up = place.at(z=(place.z + 1) % Z)
        self.down = place.at(z=(place.z + Z - 1) % Z)
        self.slots = {}

    def number(self, way, steps, part, which):
        key = (way, steps, part, which)
        if key not in self.slots:
            self.slots[key] = self.sends.slot()
        return self.slots[key]

    def reach(self, way, part):
        return 4 if (way == 0) == (part == 0) else 3

    def send(self, way, steps, part, sources):
        if steps > self.reach(way, part):
            return
        origin = (self.place.z + (Z - steps + 1 if way == 0 else steps - 1)) % Z
        targets = self.views(origin, part)
        for which, (source, target) in enumerate(zip(sources or targets, targets)):
            self.sends.start(
                self.number(way, steps, part, which),
                source,
                target,
                self.up if way == 0 else self.down,
            )

    def arrive(self, way, steps, part):
        if steps > self.reach(way, part):
            return
        origin = (self.place.z + (Z - steps if way == 0 else steps)) % Z
        for which, target in enumerate(self.views(origin, part)):
            self.sends.arrived(self.number(way, steps, part, which), target, self.up)
        self.send(way, steps + 1, part, None)


def gather_kernel(
    ql, kvl, qw, kvw, ow, all_ql, all_kvl, all_qw, all_kvw, all_ow, send_sems, recv_sems, local_sems
):
    me = Place()
    peer = me.at(y=1 - me.y)
    twin = me.at(core=1 - me.core)
    above = me.at(z=(me.z + 1) % Z)
    enter([peer, twin, above, me.at(z=(me.z + Z - 1) % Z)])
    sends = Sends(send_sems, recv_sems)

    def views(origin, part):
        row = origin * 2 + (me.y if part == 0 else 1 - me.y)
        return [all_qw.at[row], all_kvw.at[row]]

    def half(array, y):
        width = array.shape[1] // 2
        return array.at[:, pl.ds(pl.multiple_of(y * width, 128), width)]

    ring = Ring(sends, me, views)
    swap_q, swap_kv = sends.slot(), sends.slot()
    sends.start(swap_q, half(qw, 1 - me.y), all_qw.at[me.ctx], peer)
    sends.start(swap_kv, half(kvw, 1 - me.y), all_kvw.at[me.ctx], peer)
    own = [half(qw, me.y), half(kvw, me.y)]
    ring.send(0, 1, 0, own)
    ring.send(1, 1, 0, own)
    local = []
    for number, (source, target) in enumerate(
        [
            (own[0], all_qw.at[me.ctx]),
            (own[1], all_kvw.at[me.ctx]),
            (ql, all_ql.at[me.y]),
            (kvl, all_kvl.at[1 + me.y]),
            (ow, all_ow.at[me.y]),
        ]
    ):
        copy = pltpu.make_async_copy(source, target, local_sems.at[number])
        copy.start()
        local.append(copy)
    rows = ql.shape[0] // 2
    mine = pl.ds(pl.multiple_of(me.core * rows, rows), rows)
    other = pl.ds(pl.multiple_of((1 - me.core) * rows, rows), rows)
    lat_q, lat_kv = sends.slot(), sends.slot()
    sends.start(lat_kv, kvl.at[mine], all_kvl.at[1 + me.y, mine], peer)
    sends.start(lat_q, ql.at[mine], all_ql.at[me.y, mine], peer)
    sends.arrived(swap_q, all_qw.at[me.z * 2 + 1 - me.y], peer)
    sends.arrived(swap_kv, all_kvw.at[me.z * 2 + 1 - me.y], peer)
    ring.send(0, 1, 1, None)
    ring.send(1, 1, 1, None)
    out = sends.slot()
    sends.start(out, ow, all_ow.at[me.y], peer)
    ring.arrive(0, 1, 0)
    ring.arrive(1, 1, 0)
    twin_q, twin_kv, prior, twin_prior = (sends.slot() for _ in range(4))
    local[3].wait()
    sends.arrived(lat_kv, all_kvl.at[2 - me.y, mine], peer)
    sends.start(prior, all_kvl.at[2, mine], all_kvl.at[0, mine], above)
    sends.start(twin_kv, all_kvl.at[2 - me.y, mine], all_kvl.at[2 - me.y, mine], twin)
    ring.arrive(0, 1, 1)
    ring.arrive(1, 1, 1)
    sends.arrived(lat_q, all_ql.at[1 - me.y, mine], peer)
    sends.start(twin_q, all_ql.at[1 - me.y, mine], all_ql.at[1 - me.y, mine], twin)
    ring.arrive(0, 2, 0)
    ring.arrive(1, 2, 0)
    sends.arrived(prior, all_kvl.at[0, mine], above)
    sends.start(twin_prior, all_kvl.at[0, mine], all_kvl.at[0, mine], twin)
    ring.arrive(0, 2, 1)
    ring.arrive(1, 2, 1)
    for part in (0, 1):
        ring.arrive(0, 3, part)
        ring.arrive(1, 3, part)
    ring.arrive(0, 4, 0)
    ring.arrive(1, 4, 1)
    sends.arrived(twin_q, all_ql.at[1 - me.y, other], twin)
    sends.arrived(twin_kv, all_kvl.at[2 - me.y, other], twin)
    sends.arrived(twin_prior, all_kvl.at[0, other], twin)
    sends.arrived(out, all_ow.at[1 - me.y], peer)
    for number in (0, 1, 2, 4):
        local[number].wait()
    sends.drain()


def gather(ql, kvl, qw, kvw, ow):
    rows = ql.shape[0]
    ctx = lax.axis_size("ctx")
    bf16 = jnp.bfloat16
    return pl.pallas_call(
        gather_kernel,
        out_shape=[
            jax.ShapeDtypeStruct((2, rows, ql.shape[1]), bf16),
            jax.ShapeDtypeStruct((3, rows, kvl.shape[1]), bf16),
            jax.ShapeDtypeStruct((ctx, qw.shape[0], qw.shape[1] // 2), bf16),
            jax.ShapeDtypeStruct((ctx, kvw.shape[0], kvw.shape[1] // 2), bf16),
            jax.ShapeDtypeStruct((2, ow.shape[0], ow.shape[1]), bf16),
        ],
        in_specs=[ANY] * 5,
        out_specs=[ANY] * 5,
        scratch_shapes=[
            pltpu.SemaphoreType.DMA((40,)),
            pltpu.SemaphoreType.DMA((40,)),
            pltpu.SemaphoreType.DMA((5,)),
        ],
        compiler_params=pltpu.CompilerParams(collective_id=0, has_side_effects=True),
        name="gather",
    )(ql, kvl, qw, kvw, ow)


def turn(inputs, table):
    half = ROPE // 2
    swapped = jnp.concatenate([inputs[:, half:], inputs[:, :half]], axis=1)
    return inputs * table[:, :ROPE] + swapped * table[:, ROPE:]


def attend_kernel(ql, kvl, qw, kvw, gain, table, query_docs, key_docs, out, query, bias):
    tokens = ql.shape[0]
    rows = tokens // 2
    heads = qw.shape[1] // HEAD
    bf16 = jnp.bfloat16
    latent = kvl[:, :KL].astype(jnp.float32)
    scale = lax.rsqrt(jnp.mean(latent * latent, axis=-1, keepdims=True) + EPSILON)
    normed = (latent * scale * gain[...]).astype(bf16)
    key_rope = turn(kvl[:, KL:].astype(jnp.float32), table[...]).astype(bf16)
    query[...] = jnp.dot(ql[...], qw[...], preferred_element_type=jnp.float32)
    for block in range(2):
        spot_q = lax.broadcasted_iota(jnp.int32, (rows, 2 * rows), 0)
        spot_k = lax.broadcasted_iota(jnp.int32, (rows, 2 * rows), 1)
        same = query_docs[rows * block : rows * (block + 1), :] == key_docs[
            :, rows * block : rows * (block + 2)
        ]
        bias[block] = jnp.where(same & (spot_k - rows <= spot_q), 0.0, -1e30)
    for head in range(heads):
        key_value = jnp.dot(
            normed,
            kvw[:, head * (NOPE + VDIM) : (head + 1) * (NOPE + VDIM)],
            preferred_element_type=jnp.float32,
        ).astype(bf16)
        keys = jnp.concatenate([key_value[:, :NOPE], key_rope], axis=1)
        values = key_value[:, NOPE:]
        nope = query[:, head * HEAD : head * HEAD + NOPE].astype(bf16)
        rope = turn(query[:, head * HEAD + NOPE : (head + 1) * HEAD], table[rows:, :])
        queries = jnp.concatenate([nope, rope.astype(bf16)], axis=1)
        for block in range(2):
            window = slice(rows * block, rows * (block + 2))
            scores = lax.dot_general(
                queries[rows * block : rows * (block + 1)],
                keys[window],
                (((1,), (1,)), ((), ())),
                preferred_element_type=jnp.float32,
            )
            scores = scores * (HEAD ** (-0.5)) + bias[block]
            weights = jnp.exp(scores - jnp.max(scores, axis=-1, keepdims=True))
            total = jnp.sum(weights, axis=-1, keepdims=True)
            mixed = jnp.dot(
                weights.astype(bf16), values[window], preferred_element_type=jnp.float32
            )
            out[block, :, head * VDIM : (head + 1) * VDIM] = (mixed * (1.0 / total)).astype(bf16)


def attend(ql, kvl, qw, kvw, gain, table, query_docs, key_docs):
    tokens = ql.shape[0]
    heads = qw.shape[1] // HEAD
    return pl.pallas_call(
        attend_kernel,
        out_shape=jax.ShapeDtypeStruct((2, tokens // 2, heads * VDIM), jnp.bfloat16),
        in_specs=[VM] * 8,
        out_specs=VM,
        scratch_shapes=[
            pltpu.VMEM((tokens, qw.shape[1]), jnp.float32),
            pltpu.VMEM((2, tokens // 2, tokens), jnp.float32),
        ],
        compiler_params=pltpu.CompilerParams(vmem_limit_bytes=40 << 20),
        name="attend",
    )(ql, kvl, qw, kvw, gain, table, query_docs, key_docs)


def project_kernel(
    att, ow, out, every, kept, given, taken, summed, inbox, final, send_sems, recv_sems, rs_send, rs_recv, last
):
    me = Place()
    peer = me.at(y=1 - me.y)
    twin = me.at(core=1 - me.core)
    above = me.at(z=(me.z + 1) % Z)
    below = me.at(z=(me.z + Z - 1) % Z)
    goal_z = (me.chip + 4) % Z
    goal = me.at(z=goal_z, chip=me.z)
    origin = me.at(z=me.chip, chip=(me.z + 4) % Z)
    fellows = [me.at(chip=(me.chip + step) % Z) for step in range(1, Z)]
    enter([peer, twin, above, below, goal, origin] + fellows)
    sends = Sends(send_sems, recv_sems)
    depth = att.shape[2]

    def views(z, part):
        return [every.at[z, me.y if part == 0 else 1 - me.y]]

    ring = Ring(sends, me, views)
    swap = sends.slot()
    sends.start(swap, att.at[1 - me.y], every.at[me.z, me.y], peer)
    own = [att.at[me.y]]
    ring.send(0, 1, 0, own)
    ring.send(1, 1, 0, own)
    twins = [sends.slot() for _ in range(Z)]

    def product(first, second, which):
        rows = pl.ds(pl.multiple_of(me.y * depth, depth), depth)
        others = pl.ds(pl.multiple_of((1 - me.y) * depth, depth), depth)
        return jnp.dot(
            first, ow[which, rows, :], preferred_element_type=jnp.float32
        ) + jnp.dot(second, ow[which, others, :], preferred_element_type=jnp.float32)

    def tile(number, z):
        first = att[me.y] if number == 0 else every[z, me.y]
        second = every[z, 1 - me.y]
        given[number] = product(first, second, 1 - me.core).astype(jnp.bfloat16)
        sends.start(twins[number], given.at[number], taken.at[number], twin)
        kept[number % 2] = product(first, second, me.core)

    def reduce_to(number, z, start):
        target = (z + 4) % Z
        copy = pltpu.make_async_remote_copy(
            summed.at[number],
            inbox.at[me.chip],
            rs_send.at[number],
            rs_recv.at[me.chip],
            device_id=me.at(chip=target),
            device_id_type=MESH,
        )

        @pl.when(target != me.chip)
        def _():
            if start:
                copy.start()
            else:
                copy.wait_send()

        if start:

            @pl.when(target == me.chip)
            def _():
                inbox[target] = summed[number]

    def hand_over(number, z):
        sends.arrived(twins[number], taken.at[number], twin)
        summed[number] = (kept[number % 2] + taken[number].astype(jnp.float32)).astype(jnp.bfloat16)
        reduce_to(number, z, True)

    offsets = [0, 7, 1, 6, 2, 5, 3, 4]
    blocks = [(me.z + offset) % Z for offset in offsets]
    sends.arrived(swap, every.at[me.z, 1 - me.y], peer)
    ring.send(0, 1, 1, None)
    ring.send(1, 1, 1, None)
    tile(0, blocks[0])
    for steps in range(1, 4):
        for part in (0, 1):
            ring.arrive(0, steps, part)
            ring.arrive(1, steps, part)
        for number in (2 * steps - 1, 2 * steps):
            hand_over(number - 1, blocks[number - 1])
            tile(number, blocks[number])
    ring.arrive(0, 4, 0)
    ring.arrive(1, 4, 1)
    hand_over(6, blocks[6])
    tile(7, blocks[7])
    hand_over(7, blocks[7])
    for step in range(1, Z):
        source = (me.chip + step) % Z
        pltpu.make_async_remote_copy(
            inbox.at[source],
            inbox.at[source],
            rs_send.at[0],
            rs_recv.at[source],
            device_id=me.at(chip=source),
            device_id_type=MESH,
        ).wait_recv()
    total = inbox[0].astype(jnp.float32)
    for source in range(1, Z):
        total = total + inbox[source].astype(jnp.float32)
    final[0] = total.astype(jnp.bfloat16)
    move = pltpu.make_async_remote_copy(
        final.at[0], final.at[1], last.at[0], last.at[1], device_id=goal, device_id_type=MESH
    )
    move.start()
    for number in range(Z):
        reduce_to(number, blocks[number], False)
    sends.drain()
    move.wait()
    out[...] = final[1]


def project(att, ow):
    _, rows, depth = att.shape
    columns = ow.shape[2]
    bf16 = jnp.bfloat16
    return pl.pallas_call(
        project_kernel,
        out_shape=jax.ShapeDtypeStruct((rows, columns), bf16),
        in_specs=[VM] * 2,
        out_specs=VM,
        scratch_shapes=[
            pltpu.VMEM((Z, 2, rows, depth), bf16),
            pltpu.VMEM((2, rows, columns), jnp.float32),
            pltpu.VMEM((Z, rows, columns), bf16),
            pltpu.VMEM((Z, rows, columns), bf16),
            pltpu.VMEM((Z, rows, columns), bf16),
            pltpu.VMEM((Z, rows, columns), bf16),
            pltpu.VMEM((2, rows, columns), bf16),
            pltpu.SemaphoreType.DMA((32,)),
            pltpu.SemaphoreType.DMA((32,)),
            pltpu.SemaphoreType.DMA((Z,)),
            pltpu.SemaphoreType.DMA((Z,)),
            pltpu.SemaphoreType.DMA((2,)),
        ],
        compiler_params=pltpu.CompilerParams(
            collective_id=1, has_side_effects=True, vmem_limit_bytes=40 << 20
        ),
        name="project",
    )(att, ow)


def per_device(q_latent, kv_latent, kv_gain, q_weight, kv_weight, out_weight, documents):
    rows = q_latent.shape[0]
    z = lax.axis_index("ctx") // 2
    ql, kvl, qw, kvw, ow = gather(q_latent, kv_latent, q_weight, kv_weight, out_weight)
    positions = z * 2 * rows - rows + jnp.arange(3 * rows, dtype=jnp.int32)
    inverse = 10000.0 ** (-2.0 * jnp.arange(ROPE // 2, dtype=jnp.float32) / ROPE)
    angles = positions.astype(jnp.float32)[:, None] * inverse[None, :]
    cosine, sine = jnp.cos(angles), jnp.sin(angles)
    table = jnp.concatenate([cosine, cosine, -sine, sine], axis=1)
    padded = jnp.concatenate([jnp.full((rows,), -1, jnp.int32), documents])
    key_docs = lax.dynamic_slice_in_dim(padded, z * 2 * rows, 3 * rows, 0)
    att = attend(
        ql.reshape(2 * rows, -1),
        kvl.reshape(3 * rows, -1),
        qw.reshape(-1, qw.shape[2]),
        kvw.reshape(-1, kvw.shape[2]),
        kv_gain[None, :],
        table,
        key_docs[rows:, None],
        key_docs[None, :],
    )
    return project(att, ow)


def solution(mesh):
    return jax.shard_map(
        per_device,
        mesh=mesh,
        in_specs=(
            P("ctx", None),
            P("ctx", None),
            P(),
            P("ctx", "grp"),
            P("ctx", "grp"),
            P("grp", "ctx"),
            P(),
        ),
        out_specs=P("ctx", "grp"),
        check_vma=False,
    )
```

time: 417 us -> 188 us (0.45)
  the two profiles are of different devices: /device:TPU:8 before, /device:TPU:11 now
where the time goes in v1:
time: 188 us; the launch traced here: 187 us
  Pallas kernels  176 us (94%)
  local copies, waits for them, and re-layouts  9.05 us (5%)
    pallas_call x1, Pallas kernels, project(): pl.pallas_call(project_kernel, out_shape=jax.ShapeDtypeStruct((rows, colu...  91 us
    pallas_call x1, Pallas kernels, gather(): pl.pallas_call(gather_kernel, out_shape=[jax.ShapeDtypeStruct((2, rows, q...  79.5 us
    unnamed x16, local copies, waits for them, and re-layouts  7.98 us
    pallas_call x1, Pallas kernels, attend(): pl.pallas_call(attend_kernel, out_shape=jax.ShapeDtypeStruct((2, tokens /...  5.98 us

profile of v1, /device:TPU:11, one launch (start us, length us, event | category | flops | bytes accessed | tf_op | source)
XLA Modules:
  0.0 187.4 jit_solution(2015826133512756997)
XLA Ops:
  0.0 1.9 %copy.15.kvl = bf16[256,576]{1,0:T(8,128)(2,1)} copy(bf16[256,576]{0,1:T(8,128)(2,1)} %param.8) | data formatting | bytes 589824 | tf_op args[1]
  1.9 2.3 %copy.16.ow = bf16[1024,448]{1,0:T(8,128)(2,1)} copy(bf16[1024,448]{0,1:T(8,128)(2,1)} %param.12) | data formatting | bytes 1835008 | tf_op args[5]
  4.1 0.0 copy-start.6
  4.1 79.5 %gather.1 = (bf16[2,256,1536]{2,1,0:T(8,128)(2,1)}, bf16[3,256,576]{2,1,0:T(8,128)(2,1)}, bf16[16,96,768]{2,1,0:T(8,128)(2,1)}, bf16[16,32,1024]{2,1,0:T(8,128)(2,1)}, bf16[2,1024,448]{2,1,0:T(8,128)(2,1)}) custom-call(bf16[256,1536]{1,0:T(8,128)(2,1)} %ql.1, bf16[256,576]{1,0:T(8,128)(2,1)} %copy.15.kvl, bf16[96,1536]{1,0:T(8,128)(2,1)} %qw.1, ...), custom_call_target="tpu_custom_call" | custom-call | tf_op jit(solution)/shard_map/gather/pallas_call | solution.py:204
  83.6 0.0 copy-start
  83.6 0.0 copy-start.5
  83.7 1.4 multiply_cosine_fusion
  85.1 0.4 pad_maximum_fusion.table
  85.5 0.0 copy-done.6
  85.5 0.1 pad_dynamic-slice_fusion
  85.6 0.1 copy.18.query_docs
  85.8 0.0 copy-done
  85.8 0.0 copy-done.5
  85.8 0.0 copy-start.2
  85.8 1.4 copy-done.2
  87.2 0.0 copy-start.3
  87.2 1.2 copy-done.3
  88.4 0.0 copy-start.4
  88.4 1.2 copy-done.4
  89.6 0.0 copy-start.1
  89.6 6.0 %attend.1.att = bf16[2,256,512]{2,1,0:T(8,128)(2,1)S(1)} custom-call(bf16[512,1536]{1,0:T(8,128)(2,1)S(1)} %bitcast.7, bf16[768,576]{1,0:T(8,128)(2,1)S(1)} %bitcast.9, bf16[1536,768]{1,0:T(8,128)(2,1)S(1)} %bitcast.6, bf16[512,1024]{1,0:T(8,128)(2,1)S(1)} %bitcast.8, f32[1,512]{1,0:T(1,128)S(1)} %bitcast.10, f32[768,128]{1,0:T(8,128)S(1)} %pad_maximum_fusion.table, ...), custom_call_target="tpu_custom_call" | custom-call | tf_op jit(solution)/shard_map/attend/pallas_call | solution.py:279
  95.6 0.0 copy-done.1
  95.6 91.0 %project.1 = bf16[256,448]{1,0:T(8,128)(2,1)S(1)} custom-call(bf16[2,256,512]{2,1,0:T(8,128)(2,1)S(1)} %attend.1.att, bf16[2,1024,448]{2,1,0:T(8,128)(2,1)S(1)} %copy-done.1), custom_call_target="tpu_custom_call" | custom-call | tf_op jit(solution)/shard_map/project/pallas_call | solution.py:410
  186.6 0.8 copy.19
  (4 shorter events, 0.0 us)
Async XLA Ops:
  4.1 81.4 %copy-start.6 = (s32[4096]{0:T(1024)S(1)}, s32[4096]{0:T(1024)}, u32[]{:S(2)}) copy-start(s32[4096]{0:T(1024)} %param.13) | copy-start | bytes 49156
  83.6 2.2 %copy-start = (bf16[16,96,768]{2,1,0:T(8,128)(2,1)S(1)}, bf16[16,96,768]{2,1,0:T(8,128)(2,1)}, u32[]{:S(2)}) copy-start(bf16[16,96,768]{2,1,0:T(8,128)(2,1)} %get-tuple-element.12) | copy-start | bytes 7077892
  83.6 2.2 %copy-start.5 = (f32[512]{0:T(512)S(1)}, f32[512]{0:T(512)}, u32[]{:S(2)}) copy-start(f32[512]{0:T(512)} %param.9) | copy-start | bytes 6148
  85.8 1.4 copy-start.2
  87.2 1.2 copy-start.3
  88.4 1.2 copy-start.4
  89.6 6.0 %copy-start.1 = (bf16[2,1024,448]{2,1,0:T(8,128)(2,1)S(1)}, bf16[2,1024,448]{2,1,0:T(8,128)(2,1)}, u32[]{:S(2)}) copy-start(bf16[2,1024,448]{2,1,0:T(8,128)(2,1)} %get-tuple-element.14.ow) | copy-start | bytes 5505028

commit v2 on v1

--- a/solution.py
+++ b/solution.py
@@ -12,9 +12,21 @@
 HEAD = NOPE + ROPE
 Z = 8
 MESH = pl.DeviceIdType.MESH
-ANY = pl.BlockSpec(memory_space=pl.ANY)
 VM = pl.BlockSpec(memory_space=pltpu.VMEM)
 EPSILON = 1e-06
+
+
+OFFSETS = [0, 7, 1, 6, 2, 5, 3, 4]
+REDUCERS = [(1, 2), (1, 3), (1, 1), (0, 2), (1, 0), (0, 3), (0, 1), (0, 0)]
+
+
+def reducer(number, z):
+    row, column = REDUCERS[number]
+    return (z // 4 + row) % 2 * 4 + (z + column) % 4
+
+
+def choose(pick, first, second):
+    return tuple(jnp.where(pick, a, b) for a, b in zip(first, second))
 
 
 class Place:
@@ -158,7 +170,7 @@
     mine = pl.ds(pl.multiple_of(me.core * rows, rows), rows)
     other = pl.ds(pl.multiple_of((1 - me.core) * rows, rows), rows)
     lat_q, lat_kv = sends.slot(), sends.slot()
-    sends.start(lat_kv, kvl.at[mine], all_kvl.at[1 + me.y, mine], peer)
+    sends.start(lat_kv, kvl.at[:, mine], all_kvl.at[1 + me.y, :, mine], peer)
     sends.start(lat_q, ql.at[mine], all_ql.at[me.y, mine], peer)
     sends.arrived(swap_q, all_qw.at[me.z * 2 + 1 - me.y], peer)
     sends.arrived(swap_kv, all_kvw.at[me.z * 2 + 1 - me.y], peer)
@@ -170,17 +182,19 @@
     ring.arrive(1, 1, 0)
     twin_q, twin_kv, prior, twin_prior = (sends.slot() for _ in range(4))
     local[3].wait()
-    sends.arrived(lat_kv, all_kvl.at[2 - me.y, mine], peer)
-    sends.start(prior, all_kvl.at[2, mine], all_kvl.at[0, mine], above)
-    sends.start(twin_kv, all_kvl.at[2 - me.y, mine], all_kvl.at[2 - me.y, mine], twin)
+    sends.arrived(lat_kv, all_kvl.at[2 - me.y, :, mine], peer)
+    sends.start(prior, all_kvl.at[2, :, mine], all_kvl.at[0, :, mine], above)
+    sends.start(
+        twin_kv, all_kvl.at[2 - me.y, :, mine], all_kvl.at[2 - me.y, :, mine], twin
+    )
     ring.arrive(0, 1, 1)
     ring.arrive(1, 1, 1)
     sends.arrived(lat_q, all_ql.at[1 - me.y, mine], peer)
     sends.start(twin_q, all_ql.at[1 - me.y, mine], all_ql.at[1 - me.y, mine], twin)
     ring.arrive(0, 2, 0)
     ring.arrive(1, 2, 0)
-    sends.arrived(prior, all_kvl.at[0, mine], above)
-    sends.start(twin_prior, all_kvl.at[0, mine], all_kvl.at[0, mine], twin)
+    sends.arrived(prior, all_kvl.at[0, :, mine], above)
+    sends.start(twin_prior, all_kvl.at[0, :, mine], all_kvl.at[0, :, mine], twin)
     ring.arrive(0, 2, 1)
     ring.arrive(1, 2, 1)
     for part in (0, 1):
@@ -189,8 +203,8 @@
     ring.arrive(0, 4, 0)
     ring.arrive(1, 4, 1)
     sends.arrived(twin_q, all_ql.at[1 - me.y, other], twin)
-    sends.arrived(twin_kv, all_kvl.at[2 - me.y, other], twin)
-    sends.arrived(twin_prior, all_kvl.at[0, other], twin)
+    sends.arrived(twin_kv, all_kvl.at[2 - me.y, :, other], twin)
+    sends.arrived(twin_prior, all_kvl.at[0, :, other], twin)
     sends.arrived(out, all_ow.at[1 - me.y], peer)
     for number in (0, 1, 2, 4):
         local[number].wait()
@@ -205,21 +219,29 @@
         gather_kernel,
         out_shape=[
             jax.ShapeDtypeStruct((2, rows, ql.shape[1]), bf16),
-            jax.ShapeDtypeStruct((3, rows, kvl.shape[1]), bf16),
+            jax.ShapeDtypeStruct((3, kvl.shape[0], rows), bf16),
             jax.ShapeDtypeStruct((ctx, qw.shape[0], qw.shape[1] // 2), bf16),
             jax.ShapeDtypeStruct((ctx, kvw.shape[0], kvw.shape[1] // 2), bf16),
             jax.ShapeDtypeStruct((2, ow.shape[0], ow.shape[1]), bf16),
         ],
-        in_specs=[ANY] * 5,
-        out_specs=[ANY] * 5,
+        in_specs=[VM] * 5,
+        out_specs=[VM] * 5,
         scratch_shapes=[
             pltpu.SemaphoreType.DMA((40,)),
             pltpu.SemaphoreType.DMA((40,)),
             pltpu.SemaphoreType.DMA((5,)),
         ],
-        compiler_params=pltpu.CompilerParams(collective_id=0, has_side_effects=True),
+        compiler_params=pltpu.CompilerParams(
+            collective_id=0, has_side_effects=True, vmem_limit_bytes=40 << 20
+        ),
         name="gather",
     )(ql, kvl, qw, kvw, ow)
+
+
+def dot_transposed(left, right):
+    return lax.dot_general(
+        left, right, (((1,), (1,)), ((), ())), preferred_element_type=jnp.float32
+    )
 
 
 def turn(inputs, table):
@@ -233,10 +255,11 @@
     rows = tokens // 2
     heads = qw.shape[1] // HEAD
     bf16 = jnp.bfloat16
-    latent = kvl[:, :KL].astype(jnp.float32)
+    latents = jnp.concatenate([kvl[number].astype(jnp.float32).T for number in range(3)], axis=0)
+    latent = latents[:, :KL]
     scale = lax.rsqrt(jnp.mean(latent * latent, axis=-1, keepdims=True) + EPSILON)
     normed = (latent * scale * gain[...]).astype(bf16)
-    key_rope = turn(kvl[:, KL:].astype(jnp.float32), table[...]).astype(bf16)
+    key_rope = turn(latents[:, KL:], table[...]).astype(bf16)
     query[...] = jnp.dot(ql[...], qw[...], preferred_element_type=jnp.float32)
     for block in range(2):
         spot_q = lax.broadcasted_iota(jnp.int32, (rows, 2 * rows), 0)
@@ -258,12 +281,7 @@
         queries = jnp.concatenate([nope, rope.astype(bf16)], axis=1)
         for block in range(2):
             window = slice(rows * block, rows * (block + 2))
-            scores = lax.dot_general(
-                queries[rows * block : rows * (block + 1)],
-                keys[window],
-                (((1,), (1,)), ((), ())),
-                preferred_element_type=jnp.float32,
-            )
+            scores = dot_transposed(queries[rows * block : rows * (block + 1)], keys[window])
             scores = scores * (HEAD ** (-0.5)) + bias[block]
             weights = jnp.exp(scores - jnp.max(scores, axis=-1, keepdims=True))
             total = jnp.sum(weights, axis=-1, keepdims=True)
@@ -298,9 +316,12 @@
     twin = me.at(core=1 - me.core)
     above = me.at(z=(me.z + 1) % Z)
     below = me.at(z=(me.z + Z - 1) % Z)
-    goal_z = (me.chip + 4) % Z
-    goal = me.at(z=goal_z, chip=me.z)
-    origin = me.at(z=me.chip, chip=(me.z + 4) % Z)
+    goal, origin = twin, twin
+    for number, offset in enumerate(OFFSETS):
+        pick = reducer(number, me.z) == me.chip
+        goal = choose(pick, me.at(z=(me.z + offset) % Z, chip=me.z), goal)
+        pick = (me.z - me.chip + Z) % Z == offset
+        origin = choose(pick, me.at(z=me.chip, chip=reducer(number, me.chip)), origin)
     fellows = [me.at(chip=(me.chip + step) % Z) for step in range(1, Z)]
     enter([peer, twin, above, below, goal, origin] + fellows)
     sends = Sends(send_sems, recv_sems)
@@ -320,9 +341,9 @@
     def product(first, second, which):
         rows = pl.ds(pl.multiple_of(me.y * depth, depth), depth)
         others = pl.ds(pl.multiple_of((1 - me.y) * depth, depth), depth)
-        return jnp.dot(
-            first, ow[which, rows, :], preferred_element_type=jnp.float32
-        ) + jnp.dot(second, ow[which, others, :], preferred_element_type=jnp.float32)
+        return dot_transposed(first, ow[which, :, rows]) + dot_transposed(
+            second, ow[which, :, others]
+        )
 
     def tile(number, z):
         first = att[me.y] if number == 0 else every[z, me.y]
@@ -331,8 +352,8 @@
         sends.start(twins[number], given.at[number], taken.at[number], twin)
         kept[number % 2] = product(first, second, me.core)
 
-    def reduce_to(number, z, start):
-        target = (z + 4) % Z
+    def reduce_to(number, start):
+        target = reducer(number, me.z)
         copy = pltpu.make_async_remote_copy(
             summed.at[number],
             inbox.at[me.chip],
@@ -355,13 +376,35 @@
             def _():
                 inbox[target] = summed[number]
 
-    def hand_over(number, z):
+    def hand_over(number):
         sends.arrived(twins[number], taken.at[number], twin)
         summed[number] = (kept[number % 2] + taken[number].astype(jnp.float32)).astype(jnp.bfloat16)
-        reduce_to(number, z, True)
-
-    offsets = [0, 7, 1, 6, 2, 5, 3, 4]
-    blocks = [(me.z + offset) % Z for offset in offsets]
+        reduce_to(number, True)
+
+    move = pltpu.make_async_remote_copy(
+        final.at[0], final.at[1], last.at[0], last.at[1], device_id=goal, device_id_type=MESH
+    )
+
+    def finish(number):
+        @pl.when(reducer(number, me.z) == me.chip)
+        def _():
+            for step in range(1, Z):
+                source = (me.chip + step) % Z
+                pltpu.make_async_remote_copy(
+                    inbox.at[source],
+                    inbox.at[source],
+                    rs_send.at[0],
+                    rs_recv.at[source],
+                    device_id=me.at(chip=source),
+                    device_id_type=MESH,
+                ).wait_recv()
+            total = inbox[0].astype(jnp.float32)
+            for source in range(1, Z):
+                total = total + inbox[source].astype(jnp.float32)
+            final[0] = total.astype(jnp.bfloat16)
+            move.start()
+
+    blocks = [(me.z + offset) % Z for offset in OFFSETS]
     sends.arrived(swap, every.at[me.z, 1 - me.y], peer)
     ring.send(0, 1, 1, None)
     ring.send(1, 1, 1, None)
@@ -371,33 +414,19 @@
             ring.arrive(0, steps, part)
             ring.arrive(1, steps, part)
         for number in (2 * steps - 1, 2 * steps):
-            hand_over(number - 1, blocks[number - 1])
+            hand_over(number - 1)
             tile(number, blocks[number])
+            if number >= 3:
+                finish(number - 3)
     ring.arrive(0, 4, 0)
     ring.arrive(1, 4, 1)
-    hand_over(6, blocks[6])
+    hand_over(6)
     tile(7, blocks[7])
-    hand_over(7, blocks[7])
-    for step in range(1, Z):
-        source = (me.chip + step) % Z
-        pltpu.make_async_remote_copy(
-            inbox.at[source],
-            inbox.at[source],
-            rs_send.at[0],
-            rs_recv.at[source],
-            device_id=me.at(chip=source),
-            device_id_type=MESH,
-        ).wait_recv()
-    total = inbox[0].astype(jnp.float32)
-    for source in range(1, Z):
-        total = total + inbox[source].astype(jnp.float32)
-    final[0] = total.astype(jnp.bfloat16)
-    move = pltpu.make_async_remote_copy(
-        final.at[0], final.at[1], last.at[0], last.at[1], device_id=goal, device_id_type=MESH
-    )
-    move.start()
+    hand_over(7)
+    for number in range(4, Z):
+        finish(number)
     for number in range(Z):
-        reduce_to(number, blocks[number], False)
+        reduce_to(number, False)
     sends.drain()
     move.wait()
     out[...] = final[1]
@@ -405,7 +434,7 @@
 
 def project(att, ow):
     _, rows, depth = att.shape
-    columns = ow.shape[2]
+    columns = ow.shape[1]
     bf16 = jnp.bfloat16
     return pl.pallas_call(
         project_kernel,
@@ -436,7 +465,7 @@
 def per_device(q_latent, kv_latent, kv_gain, q_weight, kv_weight, out_weight, documents):
     rows = q_latent.shape[0]
     z = lax.axis_index("ctx") // 2
-    ql, kvl, qw, kvw, ow = gather(q_latent, kv_latent, q_weight, kv_weight, out_weight)
+    ql, kvl, qw, kvw, ow = gather(q_latent, kv_latent.T, q_weight, kv_weight, out_weight.T)
     positions = z * 2 * rows - rows + jnp.arange(3 * rows, dtype=jnp.int32)
     inverse = 10000.0 ** (-2.0 * jnp.arange(ROPE // 2, dtype=jnp.float32) / ROPE)
     angles = positions.astype(jnp.float32)[:, None] * inverse[None, :]
@@ -446,7 +475,7 @@
     key_docs = lax.dynamic_slice_in_dim(padded, z * 2 * rows, 3 * rows, 0)
     att = attend(
         ql.reshape(2 * rows, -1),
-        kvl.reshape(3 * rows, -1),
+        kvl,
         qw.reshape(-1, qw.shape[2]),
         kvw.reshape(-1, kvw.shape[2]),
         kv_gain[None, :],

time: 188 us -> 148 us (0.79)
  the two profiles are of different devices: /device:TPU:11 before, /device:TPU:8 now
where the time goes in v2:
time: 148 us
  Pallas kernels  144 us (97%)
  local copies, waits for them, and re-layouts  1.94 us (1%)
  other arithmetic  1.84 us (1%)
    pallas_call x1, Pallas kernels, project(): pl.pallas_call(project_kernel, out_shape=jax.ShapeDtypeStruct((rows, colu...  90.3 us
    pallas_call x1, Pallas kernels, gather(): pl.pallas_call(gather_kernel, out_shape=[jax.ShapeDtypeStruct((2, rows, q...  47.9 us
    pallas_call x1, Pallas kernels, attend(): pl.pallas_call(attend_kernel, out_shape=jax.ShapeDtypeStruct((2, tokens /...  6.11 us

profile of v2, /device:TPU:8, one launch (start us, length us, event | category | flops | bytes accessed | tf_op | source)
XLA Modules:
  0.0 148.3 jit_solution(11344830484609596178)
XLA Ops:
  0.0 0.0 copy-start
  0.0 0.0 copy-start.4
  0.0 0.0 copy-start.3
  0.0 0.0 copy-start.2
  0.0 0.0 copy-start.1
  0.1 0.9 pad_dynamic-slice_fusion
  1.0 0.1 copy.12.query_docs
  1.2 1.4 multiply_cosine_fusion
  2.6 0.0 copy-start.5
  2.6 0.4 pad_maximum_fusion.table
  3.0 0.0 copy-done
  3.0 0.0 copy-done.4
  3.0 0.0 copy-done.3
  3.0 0.0 copy-done.2
  3.0 0.0 copy-done.1
  3.1 47.9 %gather.1 = (bf16[2,256,1536]{2,1,0:T(8,128)(2,1)S(1)}, bf16[3,576,256]{2,1,0:T(8,128)(2,1)S(1)}, bf16[16,96,768]{2,1,0:T(8,128)(2,1)S(1)}, bf16[16,32,1024]{2,1,0:T(8,128)(2,1)S(1)}, bf16[2,448,1024]{2,1,0:T(8,128)(2,1)S(1)}) custom-call(bf16[256,1536]{1,0:T(8,128)(2,1)S(1)} %copy-done.1, bf16[576,256]{1,0:T(8,128)(2,1)S(1)} %bitcast.11, ...), custom_call_target="tpu_custom_call" | custom-call | tf_op jit(solution)/shard_map/gather/pallas_call | solution.py:218
  51.0 0.0 copy-done.5
  51.0 6.1 %attend.1.att = bf16[2,256,512]{2,1,0:T(8,128)(2,1)S(1)} custom-call(bf16[512,1536]{1,0:T(8,128)(2,1)S(1)} %bitcast.8, bf16[3,576,256]{2,1,0:T(8,128)(2,1)S(1)} %get-tuple-element.11.kvl, bf16[1536,768]{1,0:T(8,128)(2,1)S(1)} %bitcast.7, bf16[512,1024]{1,0:T(8,128)(2,1)S(1)} %bitcast.9, f32[1,512]{1,0:T(1,128)S(1)} %bitcast.12, ...), custom_call_target="tpu_custom_call" | custom-call | tf_op jit(solution)/shard_map/attend/pallas_call | solution.py:297
  57.1 90.3 %project.1 = bf16[256,448]{1,0:T(8,128)(2,1)S(1)} custom-call(bf16[2,256,512]{2,1,0:T(8,128)(2,1)S(1)} %attend.1.att, bf16[2,448,1024]{2,1,0:T(8,128)(2,1)S(1)} %get-tuple-element.14.ow), custom_call_target="tpu_custom_call" | custom-call | tf_op jit(solution)/shard_map/project/pallas_call | solution.py:439
  147.4 0.8 copy.13
  (4 shorter events, 0.0 us)
Async XLA Ops:
  0.0 3.0 %copy-start = (bf16[1024,448]{0,1:T(8,128)(2,1)S(1)}, bf16[1024,448]{0,1:T(8,128)(2,1)}, u32[]{:S(2)}) copy-start(bf16[1024,448]{0,1:T(8,128)(2,1)} %param.12) | copy-start | bytes 2752516
  0.0 3.0 %copy-start.4 = (bf16[32,2048]{1,0:T(8,128)(2,1)S(1)}, bf16[32,2048]{1,0:T(8,128)(2,1)}, u32[]{:S(2)}) copy-start(bf16[32,2048]{1,0:T(8,128)(2,1)} %kvw.1) | copy-start | bytes 393220
  0.0 3.0 %copy-start.3 = (bf16[96,1536]{1,0:T(8,128)(2,1)S(1)}, bf16[96,1536]{1,0:T(8,128)(2,1)}, u32[]{:S(2)}) copy-start(bf16[96,1536]{1,0:T(8,128)(2,1)} %qw.1) | copy-start | bytes 884740
  0.0 3.0 %copy-start.2 = (bf16[256,576]{0,1:T(8,128)(2,1)S(1)}, bf16[256,576]{0,1:T(8,128)(2,1)}, u32[]{:S(2)}) copy-start(bf16[256,576]{0,1:T(8,128)(2,1)} %param.8) | copy-start | bytes 884740
  0.0 3.0 %copy-start.1 = (bf16[256,1536]{1,0:T(8,128)(2,1)S(1)}, bf16[256,1536]{1,0:T(8,128)(2,1)}, u32[]{:S(2)}) copy-start(bf16[256,1536]{1,0:T(8,128)(2,1)} %ql.1) | copy-start | bytes 2359300
  2.6 48.4 %copy-start.5 = (f32[512]{0:T(512)S(1)}, f32[512]{0:T(512)}, u32[]{:S(2)}) copy-start(f32[512]{0:T(512)} %param.9) | copy-start | bytes 6148

commit v3 on v2

--- a/solution.py
+++ b/solution.py
@@ -17,16 +17,6 @@
 
 
 OFFSETS = [0, 7, 1, 6, 2, 5, 3, 4]
-REDUCERS = [(1, 2), (1, 3), (1, 1), (0, 2), (1, 0), (0, 3), (0, 1), (0, 0)]
-
-
-def reducer(number, z):
-    row, column = REDUCERS[number]
-    return (z // 4 + row) % 2 * 4 + (z + column) % 4
-
-
-def choose(pick, first, second):
-    return tuple(jnp.where(pick, a, b) for a, b in zip(first, second))
 
 
 class Place:
@@ -309,23 +299,36 @@
 
 
 def project_kernel(
-    att, ow, out, every, kept, given, taken, summed, inbox, final, send_sems, recv_sems, rs_send, rs_recv, last
+    att,
+    ow,
+    out,
+    every,
+    kept,
+    given,
+    taken,
+    summed,
+    inbox,
+    reduced,
+    moved,
+    final,
+    send_sems,
+    recv_sems,
+    part_send,
+    part_recv,
+    move_send,
+    move_recv,
+    last,
 ):
     me = Place()
     peer = me.at(y=1 - me.y)
     twin = me.at(core=1 - me.core)
-    above = me.at(z=(me.z + 1) % Z)
-    below = me.at(z=(me.z + Z - 1) % Z)
-    goal, origin = twin, twin
-    for number, offset in enumerate(OFFSETS):
-        pick = reducer(number, me.z) == me.chip
-        goal = choose(pick, me.at(z=(me.z + offset) % Z, chip=me.z), goal)
-        pick = (me.z - me.chip + Z) % Z == offset
-        origin = choose(pick, me.at(z=me.chip, chip=reducer(number, me.chip)), origin)
     fellows = [me.at(chip=(me.chip + step) % Z) for step in range(1, Z)]
-    enter([peer, twin, above, below, goal, origin] + fellows)
+    column = [me.at(z=(me.z + step) % Z) for step in range(1, Z)]
+    enter([peer, twin] + fellows + column)
     sends = Sends(send_sems, recv_sems)
     depth = att.shape[2]
+    rows = out.shape[0] // Z
+    mine = pl.ds(pl.multiple_of(me.chip * rows, rows), rows)
 
     def views(z, part):
         return [every.at[z, me.y if part == 0 else 1 - me.y]]
@@ -338,103 +341,121 @@
     ring.send(1, 1, 0, own)
     twins = [sends.slot() for _ in range(Z)]
 
+    def remote(source, target, send, recv, device):
+        return pltpu.make_async_remote_copy(
+            source, target, send, recv, device_id=device, device_id_type=MESH
+        )
+
     def product(first, second, which):
-        rows = pl.ds(pl.multiple_of(me.y * depth, depth), depth)
-        others = pl.ds(pl.multiple_of((1 - me.y) * depth, depth), depth)
-        return dot_transposed(first, ow[which, :, rows]) + dot_transposed(
-            second, ow[which, :, others]
-        )
-
-    def tile(number, z):
+        near = pl.ds(pl.multiple_of(me.y * depth, depth), depth)
+        far = pl.ds(pl.multiple_of((1 - me.y) * depth, depth), depth)
+        return dot_transposed(first, ow[which, :, near]) + dot_transposed(second, ow[which, :, far])
+
+    def tile(number):
+        z = (me.z + OFFSETS[number]) % Z
         first = att[me.y] if number == 0 else every[z, me.y]
         second = every[z, 1 - me.y]
         given[number] = product(first, second, 1 - me.core).astype(jnp.bfloat16)
         sends.start(twins[number], given.at[number], taken.at[number], twin)
         kept[number % 2] = product(first, second, me.core)
 
-    def reduce_to(number, start):
-        target = reducer(number, me.z)
-        copy = pltpu.make_async_remote_copy(
-            summed.at[number],
-            inbox.at[me.chip],
-            rs_send.at[number],
-            rs_recv.at[me.chip],
-            device_id=me.at(chip=target),
-            device_id_type=MESH,
-        )
-
-        @pl.when(target != me.chip)
-        def _():
-            if start:
-                copy.start()
-            else:
-                copy.wait_send()
-
-        if start:
-
-            @pl.when(target == me.chip)
-            def _():
-                inbox[target] = summed[number]
-
-    def hand_over(number):
+    def spread(number):
         sends.arrived(twins[number], taken.at[number], twin)
         summed[number] = (kept[number % 2] + taken[number].astype(jnp.float32)).astype(jnp.bfloat16)
-        reduce_to(number, True)
-
-    move = pltpu.make_async_remote_copy(
-        final.at[0], final.at[1], last.at[0], last.at[1], device_id=goal, device_id_type=MESH
-    )
+        for step in range(1, Z):
+            chip = (me.chip + step) % Z
+            part = pl.ds(pl.multiple_of(chip * rows, rows), rows)
+            remote(
+                summed.at[number, part],
+                inbox.at[number, step - 1],
+                part_send.at[number],
+                part_recv.at[number],
+                fellows[step - 1],
+            ).start()
+
+    def parts(number):
+        return remote(
+            inbox.at[number], inbox.at[number], part_send.at[number], part_recv.at[number], peer
+        )
+
+    def move(number):
+        return remote(
+            reduced.at[number],
+            moved.at[number],
+            move_send.at[number],
+            move_recv.at[number],
+            me.at(z=(me.z + OFFSETS[number]) % Z),
+        )
 
     def finish(number):
-        @pl.when(reducer(number, me.z) == me.chip)
+        parts(number).wait_recv()
+        total = summed[number, mine, :].astype(jnp.float32)
+        for source in range(Z - 1):
+            total = total + inbox[number, source].astype(jnp.float32)
+        if number == 0:
+            moved[0] = total.astype(jnp.bfloat16)
+        else:
+            reduced[number] = total.astype(jnp.bfloat16)
+            move(number).start()
+
+    def deliver(number):
+        if number:
+            move(number).wait_recv()
+        chip = (me.z + Z - OFFSETS[number]) % Z
+
+        @pl.when(chip == me.chip)
         def _():
-            for step in range(1, Z):
-                source = (me.chip + step) % Z
-                pltpu.make_async_remote_copy(
-                    inbox.at[source],
-                    inbox.at[source],
-                    rs_send.at[0],
-                    rs_recv.at[source],
-                    device_id=me.at(chip=source),
-                    device_id_type=MESH,
-                ).wait_recv()
-            total = inbox[0].astype(jnp.float32)
-            for source in range(1, Z):
-                total = total + inbox[source].astype(jnp.float32)
-            final[0] = total.astype(jnp.bfloat16)
-            move.start()
-
-    blocks = [(me.z + offset) % Z for offset in OFFSETS]
+            final[mine, :] = moved[number]
+
+        @pl.when(chip != me.chip)
+        def _():
+            remote(
+                moved.at[number], final.at[mine], last.at[0], last.at[1], me.at(chip=chip)
+            ).start()
+
     sends.arrived(swap, every.at[me.z, 1 - me.y], peer)
     ring.send(0, 1, 1, None)
     ring.send(1, 1, 1, None)
-    tile(0, blocks[0])
+    tile(0)
     for steps in range(1, 4):
         for part in (0, 1):
             ring.arrive(0, steps, part)
             ring.arrive(1, steps, part)
         for number in (2 * steps - 1, 2 * steps):
-            hand_over(number - 1)
-            tile(number, blocks[number])
+            spread(number - 1)
+            tile(number)
             if number >= 3:
                 finish(number - 3)
+    spread(6)
+    finish(4)
+    for number in range(3):
+        deliver(number)
     ring.arrive(0, 4, 0)
     ring.arrive(1, 4, 1)
-    hand_over(6)
-    tile(7, blocks[7])
-    hand_over(7)
-    for number in range(4, Z):
-        finish(number)
+    tile(7)
+    finish(5)
+    spread(7)
+    finish(6)
+    deliver(3)
+    deliver(4)
+    finish(7)
+    deliver(5)
+    deliver(6)
+    deliver(7)
+    sends.drain()
     for number in range(Z):
-        reduce_to(number, False)
-    sends.drain()
-    move.wait()
-    out[...] = final[1]
+        parts(number).wait_send()
+        if number:
+            move(number).wait_send()
+    everyone = final.at[pl.ds(0, rows * (Z - 1))]
+    remote(everyone, everyone, last.at[0], last.at[1], peer).wait()
+    out[...] = final[...]
 
 
 def project(att, ow):
     _, rows, depth = att.shape
     columns = ow.shape[1]
+    part = rows // Z
     bf16 = jnp.bfloat16
     return pl.pallas_call(
         project_kernel,
@@ -447,10 +468,14 @@
             pltpu.VMEM((Z, rows, columns), bf16),
             pltpu.VMEM((Z, rows, columns), bf16),
             pltpu.VMEM((Z, rows, columns), bf16),
-            pltpu.VMEM((Z, rows, columns), bf16),
-            pltpu.VMEM((2, rows, columns), bf16),
+            pltpu.VMEM((Z, Z - 1, part, columns), bf16),
+            pltpu.VMEM((Z, part, columns), bf16),
+            pltpu.VMEM((Z, part, columns), bf16),
+            pltpu.VMEM((rows, columns), bf16),
             pltpu.SemaphoreType.DMA((32,)),
             pltpu.SemaphoreType.DMA((32,)),
+            pltpu.SemaphoreType.DMA((Z,)),
+            pltpu.SemaphoreType.DMA((Z,)),
             pltpu.SemaphoreType.DMA((Z,)),
             pltpu.SemaphoreType.DMA((Z,)),
             pltpu.SemaphoreType.DMA((2,)),

time: 148 us -> 126 us (0.85)
  Pallas kernels: 144 us -> 122 us
    pallas_call x1, Pallas kernels: 90.3 us -> 67.5 us  [project(): pl.pallas_call(project_kernel, out_shape=jax.ShapeDtypeStruct((rows, colu...]
where the time goes in v3:
time: 126 us; the launch traced here: 125 us
  Pallas kernels  122 us (97%)
  local copies, waits for them, and re-layouts  1.94 us (2%)
  other arithmetic  1.84 us (1%)
    pallas_call x1, Pallas kernels, project(): pl.pallas_call(project_kernel, out_shape=jax.ShapeDtypeStruct((rows, colu...  67.5 us
    pallas_call x1, Pallas kernels, gather(): pl.pallas_call(gather_kernel, out_shape=[jax.ShapeDtypeStruct((2, rows, q...  47.9 us
    pallas_call x1, Pallas kernels, attend(): pl.pallas_call(attend_kernel, out_shape=jax.ShapeDtypeStruct((2, tokens /...  6.11 us

profile of v3, /device:TPU:8, one launch (start us, length us, event | category | flops | bytes accessed | tf_op | source)
XLA Modules:
  0.0 125.4 jit_solution(7995135423913652169)
XLA Ops:
  0.0 0.0 copy-start
  0.0 0.0 copy-start.4
  0.0 0.0 copy-start.3
  0.0 0.0 copy-start.2
  0.0 0.0 copy-start.1
  0.1 0.9 pad_dynamic-slice_fusion
  1.0 0.1 copy.12.query_docs
  1.2 1.4 %multiply_cosine_fusion = (f32[768,32]{1,0:T(8,128)S(1)}, f32[768,32]{1,0:T(8,128)S(1)}, f32[768,32]{1,0:T(8,128)S(1)}) fusion(f32[768]{0:T(1024)S(1)} %add_convert_fusion, f32[32]{0:T(128)S(1)} %multiply_power_fusion), kind=kLoop, calls=%fused_computation.1 | loop fusion | flops 49152 | bytes 298112 | tf_op jit(solution)/shard_map/cos | solution.py:497
  2.6 0.0 copy-start.5
  2.6 0.4 pad_maximum_fusion.table
  3.0 0.0 copy-done
  3.0 0.0 copy-done.4
  3.0 0.0 copy-done.3
  3.0 0.0 copy-done.2
  3.0 0.0 copy-done.1
  3.1 47.9 %gather.1 = (bf16[2,256,1536]{2,1,0:T(8,128)(2,1)S(1)}, bf16[3,576,256]{2,1,0:T(8,128)(2,1)S(1)}, bf16[16,96,768]{2,1,0:T(8,128)(2,1)S(1)}, bf16[16,32,1024]{2,1,0:T(8,128)(2,1)S(1)}, bf16[2,448,1024]{2,1,0:T(8,128)(2,1)S(1)}) custom-call(bf16[256,1536]{1,0:T(8,128)(2,1)S(1)} %copy-done.1, bf16[576,256]{1,0:T(8,128)(2,1)S(1)} %bitcast.11, ...), custom_call_target="tpu_custom_call" | custom-call | tf_op jit(solution)/shard_map/gather/pallas_call | solution.py:208
  51.0 0.0 copy-done.5
  51.0 6.1 %attend.1.att = bf16[2,256,512]{2,1,0:T(8,128)(2,1)S(1)} custom-call(bf16[512,1536]{1,0:T(8,128)(2,1)S(1)} %bitcast.8, bf16[3,576,256]{2,1,0:T(8,128)(2,1)S(1)} %get-tuple-element.11.kvl, bf16[1536,768]{1,0:T(8,128)(2,1)S(1)} %bitcast.7, bf16[512,1024]{1,0:T(8,128)(2,1)S(1)} %bitcast.9, f32[1,512]{1,0:T(1,128)S(1)} %bitcast.12, ...), custom_call_target="tpu_custom_call" | custom-call | tf_op jit(solution)/shard_map/attend/pallas_call | solution.py:287
  57.1 67.5 %project.1 = bf16[256,448]{1,0:T(8,128)(2,1)S(1)} custom-call(bf16[2,256,512]{2,1,0:T(8,128)(2,1)S(1)} %attend.1.att, bf16[2,448,1024]{2,1,0:T(8,128)(2,1)S(1)} %get-tuple-element.14.ow), custom_call_target="tpu_custom_call" | custom-call | tf_op jit(solution)/shard_map/project/pallas_call | solution.py:460
  124.6 0.8 copy.13
  (4 shorter events, 0.0 us)
Async XLA Ops:
  0.0 3.0 %copy-start = (bf16[1024,448]{0,1:T(8,128)(2,1)S(1)}, bf16[1024,448]{0,1:T(8,128)(2,1)}, u32[]{:S(2)}) copy-start(bf16[1024,448]{0,1:T(8,128)(2,1)} %param.12) | copy-start | bytes 2752516
  0.0 3.0 %copy-start.4 = (bf16[32,2048]{1,0:T(8,128)(2,1)S(1)}, bf16[32,2048]{1,0:T(8,128)(2,1)}, u32[]{:S(2)}) copy-start(bf16[32,2048]{1,0:T(8,128)(2,1)} %kvw.1) | copy-start | bytes 393220
  0.0 3.0 %copy-start.3 = (bf16[96,1536]{1,0:T(8,128)(2,1)S(1)}, bf16[96,1536]{1,0:T(8,128)(2,1)}, u32[]{:S(2)}) copy-start(bf16[96,1536]{1,0:T(8,128)(2,1)} %qw.1) | copy-start | bytes 884740
  0.0 3.0 %copy-start.2 = (bf16[256,576]{0,1:T(8,128)(2,1)S(1)}, bf16[256,576]{0,1:T(8,128)(2,1)}, u32[]{:S(2)}) copy-start(bf16[256,576]{0,1:T(8,128)(2,1)} %param.8) | copy-start | bytes 884740
  0.0 3.0 %copy-start.1 = (bf16[256,1536]{1,0:T(8,128)(2,1)S(1)}, bf16[256,1536]{1,0:T(8,128)(2,1)}, u32[]{:S(2)}) copy-start(bf16[256,1536]{1,0:T(8,128)(2,1)} %ql.1) | copy-start | bytes 2359300
  2.6 48.4 %copy-start.5 = (f32[512]{0:T(512)S(1)}, f32[512]{0:T(512)}, u32[]{:S(2)}) copy-start(f32[512]{0:T(512)} %param.9) | copy-start | bytes 6148

commit v4 on v3

v4 whole, which is shorter than its diff:
```python
import jax
import jax.numpy as jnp
from jax import lax
from jax.experimental import pallas as pl
from jax.experimental.pallas import tpu as pltpu
from jax.sharding import PartitionSpec as P

KL = 512
NOPE = 128
ROPE = 64
VDIM = 128
HEAD = NOPE + ROPE
Z = 8
MESH = pl.DeviceIdType.MESH
VM = pl.BlockSpec(memory_space=pltpu.VMEM)
EPSILON = 1e-06
OFFSETS = [0, 7, 1, 6, 2, 5, 3, 4]


class Place:
    def __init__(self):
        ctx = lax.axis_index("ctx")
        grp = lax.axis_index("grp")
        self.ctx = ctx
        self.z = ctx // 2
        self.y = ctx % 2
        self.chip = grp // 2
        self.core = grp % 2

    def at(self, z=None, y=None, chip=None, core=None):
        z = self.z if z is None else z
        y = self.y if y is None else y
        chip = self.chip if chip is None else chip
        core = self.core if core is None else core
        return (z * 2 + y, chip * 2 + core)


class Sends:
    def __init__(self, send_sems, recv_sems):
        self.send_sems = send_sems
        self.recv_sems = recv_sems
        self.used = 0
        self.started = []

    def slot(self):
        self.used += 1
        return self.used - 1

    def make(self, number, source, target, device):
        return pltpu.make_async_remote_copy(
            source,
            target,
            self.send_sems.at[number],
            self.recv_sems.at[number],
            device_id=device,
            device_id_type=MESH,
        )

    def start(self, number, source, target, device):
        copy = self.make(number, source, target, device)
        copy.start()
        self.started.append(copy)

    def arrived(self, number, target, device):
        self.make(number, target, target, device).wait_recv()

    def drain(self):
        for copy in self.started:
            copy.wait_send()


def enter(devices):
    barrier = pltpu.get_barrier_semaphore()
    for device in devices:
        pl.semaphore_signal(barrier, inc=1, device_id=device, device_id_type=MESH)
    pl.semaphore_wait(barrier, len(devices))


class Ring:
    def __init__(self, sends, place, views):
        self.sends = sends
        self.place = place
        self.views = views
        self.up = place.at(z=(place.z + 1) % Z)
        self.down = place.at(z=(place.z + Z - 1) % Z)
        self.slots = {}

    def number(self, way, steps, part, which):
        key = (way, steps, part, which)
        if key not in self.slots:
            self.slots[key] = self.sends.slot()
        return self.slots[key]

    def reach(self, way, part):
        return 4 if (way == 0) == (part == 0) else 3

    def send(self, way, steps, part, sources):
        if steps > self.reach(way, part):
            return
        origin = (self.place.z + (Z - steps + 1 if way == 0 else steps - 1)) % Z
        targets = self.views(origin, part)
        for which, (source, target) in enumerate(zip(sources or targets, targets)):
            self.sends.start(
                self.number(way, steps, part, which),
                source,
                target,
                self.up if way == 0 else self.down,
            )

    def arrive(self, way, steps, part):
        if steps > self.reach(way, part):
            return
        origin = (self.place.z + (Z - steps if way == 0 else steps)) % Z
        for which, target in enumerate(self.views(origin, part)):
            self.sends.arrived(self.number(way, steps, part, which), target, self.up)
        self.send(way, steps + 1, part, None)


def dot(left, right):
    return jnp.dot(left, right, preferred_element_type=jnp.float32)


def dot_transposed(left, right):
    return lax.dot_general(
        left, right, (((1,), (1,)), ((), ())), preferred_element_type=jnp.float32
    )


def turn(inputs, table):
    half = ROPE // 2
    swapped = jnp.concatenate([inputs[:, half:], inputs[:, :half]], axis=1)
    return inputs * table[:, :ROPE] + swapped * table[:, ROPE:]


def layer_kernel(
    ql,
    kvl,
    qw,
    kvw,
    ow,
    gain,
    inverse,
    documents,
    out,
    all_ql,
    all_kvl,
    all_qw,
    all_kvw,
    all_ow,
    docs,
    table,
    bias,
    normed,
    key_rope,
    query,
    key_value,
    att,
    every,
    kept,
    given,
    taken,
    summed,
    inbox,
    reduced,
    moved,
    final,
    send_sems,
    recv_sems,
    local_sems,
    part_send,
    part_recv,
    move_send,
    move_recv,
    last,
):
    bf16 = jnp.bfloat16
    me = Place()
    peer = me.at(y=1 - me.y)
    twin = me.at(core=1 - me.core)
    fellows = [me.at(chip=(me.chip + step) % Z) for step in range(1, Z)]
    column = [me.at(z=(me.z + step) % Z) for step in range(1, Z)]
    above = column[0]
    enter([peer, twin] + fellows + column)
    sends = Sends(send_sems, recv_sems)
    tokens = ql.shape[0]
    deep_q, deep_kv = qw.shape[0], kvw.shape[0]
    wide_q, wide_kv = qw.shape[1] // 4, kvw.shape[1] // 4
    depth = att.shape[3]
    rows = out.shape[0] // Z
    mine = pl.ds(pl.multiple_of(me.chip * rows, rows), rows)

    def remote(source, target, send, recv, device):
        return pltpu.make_async_remote_copy(
            source, target, send, recv, device_id=device, device_id_type=MESH
        )

    def slab(array, pair, row, deep):
        return array.at[pair, pl.ds(pl.multiple_of(row * deep, deep), deep)]

    def weight_views(pair):
        def views(origin, part):
            row = origin * 2 + (me.y if part == 0 else 1 - me.y)
            return [slab(all_qw, pair, row, deep_q), slab(all_kvw, pair, row, deep_kv)]

        return views

    def cut(y, pair):
        number = y * 2 + pair
        return [
            qw.at[:, pl.ds(pl.multiple_of(number * wide_q, 128), wide_q)],
            kvw.at[:, pl.ds(pl.multiple_of(number * wide_kv, 128), wide_kv)],
        ]

    def attended_views(pair):
        def views(origin, part):
            return [every.at[pair, origin, me.y if part == 0 else 1 - me.y]]

        return views

    weights = [Ring(sends, me, weight_views(pair)) for pair in range(2)]
    results = [Ring(sends, me, attended_views(pair)) for pair in range(2)]
    swaps = [[sends.slot(), sends.slot()] for _ in range(2)]
    backs = [sends.slot() for _ in range(2)]
    twins = [sends.slot() for _ in range(Z)]
    lat_q, lat_kv, twin_q, twin_kv, prior, twin_prior, swap_out = (sends.slot() for _ in range(7))

    def both(ring, steps, part):
        ring.arrive(0, steps, part)
        ring.arrive(1, steps, part)

    def begin(ring, part, sources):
        ring.send(0, 1, part, sources)
        ring.send(1, 1, part, sources)

    def swap_weights(pair):
        for number, source, target in zip(
            swaps[pair], cut(1 - me.y, pair), weights[pair].views(me.z, 0)
        ):
            sends.start(number, source, target, peer)

    def swapped_weights(pair):
        for number, target in zip(swaps[pair], weights[pair].views(me.z, 1)):
            sends.arrived(number, target, peer)

    half = tokens // 2
    near = pl.ds(pl.multiple_of(me.core * half, half), half)
    far = pl.ds(pl.multiple_of((1 - me.core) * half, half), half)

    def make_tables():
        docs[:, :tokens] = jnp.full((1, tokens), -1.0, jnp.float32)
        docs[:, tokens:] = documents[...].astype(jnp.float32)
        key_docs = docs[:, pl.ds(pl.multiple_of(me.z * 2 * tokens, 128), 3 * tokens)]
        query_docs = jnp.broadcast_to(key_docs[:, tokens:], (128, 2 * tokens)).T
        for block in range(2):
            shape = (tokens, 2 * tokens)
            spot_q = lax.broadcasted_iota(jnp.int32, shape, 0)
            spot_k = lax.broadcasted_iota(jnp.int32, shape, 1)
            same = (
                query_docs[tokens * block : tokens * (block + 1), :1]
                == key_docs[:, tokens * block : tokens * (block + 2)]
            )
            bias[block] = jnp.where(same & (spot_k - tokens <= spot_q), 0.0, -1e30)
        first = me.z * 2 * tokens - tokens
        spots = (first + lax.broadcasted_iota(jnp.int32, (3 * tokens, 128), 0)).astype(jnp.float32)
        angles = spots * inverse[...]
        lane = lax.broadcasted_iota(jnp.int32, (3 * tokens, 128), 1)
        sine = jnp.sin(angles)
        table[...] = jnp.where(
            lane < ROPE, jnp.cos(angles), jnp.where(lane < ROPE + ROPE // 2, -sine, sine)
        )

    def make_keys():
        latents = jnp.concatenate(
            [all_kvl[number].astype(jnp.float32).T for number in range(3)], axis=0
        )
        latent = latents[:, :KL]
        scale = lax.rsqrt(jnp.mean(latent * latent, axis=-1, keepdims=True) + EPSILON)
        normed[...] = (latent * scale * gain[...]).astype(bf16)
        key_rope[...] = turn(latents[:, KL:], table[...]).astype(bf16)

    def make_pair(pair):
        for block in range(2):
            query[tokens * block : tokens * (block + 1), :] = dot(all_ql[block], all_qw[pair])
        key_value[...] = dot(normed[...], all_kvw[pair]).astype(bf16)

    def attend(pair, head):
        start = head * (NOPE + VDIM)
        keys = jnp.concatenate([key_value[:, start : start + NOPE], key_rope[...]], axis=1)
        values = key_value[:, start + NOPE : start + NOPE + VDIM]
        nope = query[:, head * HEAD : head * HEAD + NOPE].astype(bf16)
        rope = turn(query[:, head * HEAD + NOPE : (head + 1) * HEAD], table[tokens:, :])
        queries = jnp.concatenate([nope, rope.astype(bf16)], axis=1)
        for block in range(2):
            window = slice(tokens * block, tokens * (block + 2))
            scores = dot_transposed(queries[tokens * block : tokens * (block + 1)], keys[window])
            scores = scores * (HEAD ** (-0.5)) + bias[block]
            powers = jnp.exp(scores - jnp.max(scores, axis=-1, keepdims=True))
            total = jnp.sum(powers, axis=-1, keepdims=True)
            mixed = dot(powers.astype(bf16), values[window]) * (1.0 / total)
            att[pair, block, :, head * VDIM : (head + 1) * VDIM] = mixed.astype(bf16)

    def swap_attended(pair):
        sends.start(backs[pair], att.at[pair, 1 - me.y], every.at[pair, me.z, me.y], peer)

    def swapped_attended(pair):
        sends.arrived(backs[pair], every.at[pair, me.z, 1 - me.y], peer)

    def product(number, z, which):
        total = None
        for y in (me.y, 1 - me.y):
            for pair in range(2):
                if number == 0 and y is me.y:
                    left = att[pair, y]
                else:
                    left = every[pair, z, y]
                part = pl.ds(pl.multiple_of((y * 2 + pair) * depth, depth), depth)
                term = dot_transposed(left, all_ow[which, :, part])
                total = term if total is None else total + term
        return total

    def tile(number):
        z = (me.z + OFFSETS[number]) % Z
        given[number] = product(number, z, 1 - me.core).astype(bf16)
        sends.start(twins[number], given.at[number], taken.at[number], twin)
        kept[number % 2] = product(number, z, me.core)

    def spread(number):
        sends.arrived(twins[number], taken.at[number], twin)
        summed[number] = (kept[number % 2] + taken[number].astype(jnp.float32)).astype(bf16)
        for step in range(1, Z):
            chip = (me.chip + step) % Z
            part = pl.ds(pl.multiple_of(chip * rows, rows), rows)
            remote(
                summed.at[number, part],
                inbox.at[number, step - 1],
                part_send.at[number],
                part_recv.at[number],
                fellows[step - 1],
            ).start()

    def parts(number):
        return remote(
            inbox.at[number], inbox.at[number], part_send.at[number], part_recv.at[number], peer
        )

    def move(number):
        return remote(
            reduced.at[number],
            moved.at[number],
            move_send.at[number],
            move_recv.at[number],
            me.at(z=(me.z + OFFSETS[number]) % Z),
        )

    def finish(number):
        parts(number).wait_recv()
        total = summed[number, mine, :].astype(jnp.float32)
        for source in range(Z - 1):
            total = total + inbox[number, source].astype(jnp.float32)
        if number == 0:
            moved[0] = total.astype(bf16)
        else:
            reduced[number] = total.astype(bf16)
            move(number).start()

    def deliver(number):
        if number:
            move(number).wait_recv()
        chip = (me.z + Z - OFFSETS[number]) % Z

        @pl.when(chip == me.chip)
        def _():
            final[mine, :] = moved[number]

        @pl.when(chip != me.chip)
        def _():
            remote(
                moved.at[number], final.at[mine], last.at[0], last.at[1], me.at(chip=chip)
            ).start()

    swap_weights(0)
    begin(weights[0], 0, cut(me.y, 0))
    local = []
    for source, target in [
        (cut(me.y, 0)[0], weights[0].views(me.z, 0)[0]),
        (cut(me.y, 0)[1], weights[0].views(me.z, 0)[1]),
        (cut(me.y, 1)[0], weights[1].views(me.z, 0)[0]),
        (cut(me.y, 1)[1], weights[1].views(me.z, 0)[1]),
        (kvl, all_kvl.at[1 + me.y]),
        (ql, all_ql.at[me.y]),
        (ow, all_ow.at[me.y]),
    ]:
        copy = pltpu.make_async_copy(source, target, local_sems.at[len(local)])
        copy.start()
        local.append(copy)
    sends.start(lat_kv, kvl.at[:, near], all_kvl.at[1 + me.y, :, near], peer)
    sends.start(lat_q, ql.at[near], all_ql.at[me.y, near], peer)
    swapped_weights(0)
    begin(weights[0], 1, None)
    swap_weights(1)
    make_tables()
    both(weights[0], 1, 0)
    sends.start(swap_out, ow, all_ow.at[me.y], peer)
    local[4].wait()
    sends.arrived(lat_kv, all_kvl.at[2 - me.y, :, near], peer)
    sends.start(prior, all_kvl.at[2, :, near], all_kvl.at[0, :, near], above)
    sends.start(
        twin_kv, all_kvl.at[2 - me.y, :, near], all_kvl.at[2 - me.y, :, near], twin
    )
    both(weights[0], 1, 1)
    sends.arrived(lat_q, all_ql.at[1 - me.y, near], peer)
    sends.start(twin_q, all_ql.at[1 - me.y, near], all_ql.at[1 - me.y, near], twin)
    both(weights[0], 2, 0)
    sends.arrived(prior, all_kvl.at[0, :, near], above)
    sends.start(twin_prior, all_kvl.at[0, :, near], all_kvl.at[0, :, near], twin)
    both(weights[0], 2, 1)
    both(weights[0], 3, 0)
    both(weights[0], 3, 1)
    begin(weights[1], 0, cut(me.y, 1))
    swapped_weights(1)
    begin(weights[1], 1, None)
    sends.arrived(twin_kv, all_kvl.at[2 - me.y, :, far], twin)
    sends.arrived(twin_prior, all_kvl.at[0, :, far], twin)
    make_keys()
    both(weights[0], 4, 0)
    both(weights[0], 4, 1)
    sends.arrived(twin_q, all_ql.at[1 - me.y, far], twin)
    for number in (0, 1, 5):
        local[number].wait()
    make_pair(0)
    both(weights[1], 1, 0)
    both(weights[1], 1, 1)
    attend(0, 0)
    both(weights[1], 2, 0)
    attend(0, 1)
    swap_attended(0)
    begin(results[0], 0, [att.at[0, me.y]])
    both(weights[1], 2, 1)
    both(weights[1], 3, 0)
    both(weights[1], 3, 1)
    swapped_attended(0)
    begin(results[0], 1, None)
    both(weights[1], 4, 0)
    both(weights[1], 4, 1)
    for number in (2, 3):
        local[number].wait()
    make_pair(1)
    both(results[0], 1, 0)
    attend(1, 0)
    both(results[0], 1, 1)
    attend(1, 1)
    swap_attended(1)
    begin(results[1], 0, [att.at[1, me.y]])
    both(results[0], 2, 0)
    both(results[0], 2, 1)
    swapped_attended(1)
    begin(results[1], 1, None)
    local[6].wait()
    sends.arrived(swap_out, all_ow.at[1 - me.y], peer)
    tile(0)
    for steps in range(1, 4):
        for part in (0, 1):
            if steps == 1:
                both(results[0], 3, part)
            both(results[1], steps, part)
            if steps == 2:
                both(results[0], 4, part)
        for number in (2 * steps - 1, 2 * steps):
            spread(number - 1)
            tile(number)
            if number >= 3:
                finish(number - 3)
    spread(6)
    finish(4)
    for number in range(3):
        deliver(number)
    both(results[1], 4, 0)
    both(results[1], 4, 1)
    tile(7)
    finish(5)
    spread(7)
    finish(6)
    deliver(3)
    deliver(4)
    finish(7)
    deliver(5)
    deliver(6)
    deliver(7)
    sends.drain()
    for number in range(Z):
        parts(number).wait_send()
        if number:
            move(number).wait_send()
    everyone = final.at[pl.ds(0, rows * (Z - 1))]
    remote(everyone, everyone, last.at[0], last.at[1], peer).wait()
    out[...] = final[...]


def per_device(q_latent, kv_latent, kv_gain, q_weight, kv_weight, out_weight, documents):
    tokens = q_latent.shape[0]
    columns = out_weight.shape[1]
    ctx = lax.axis_size("ctx")
    wide_q, wide_kv = q_weight.shape[1] // 4, kv_weight.shape[1] // 4
    depth = 2 * VDIM
    part = tokens // Z
    bf16, f32 = jnp.bfloat16, jnp.float32
    spot = jnp.arange(128, dtype=f32) % (ROPE // 2)
    inverse = (10000.0 ** (-2.0 * spot / ROPE))[None, :]
    return pl.pallas_call(
        layer_kernel,
        out_shape=jax.ShapeDtypeStruct((tokens, columns), bf16),
        in_specs=[VM] * 8,
        out_specs=VM,
        scratch_shapes=[
            pltpu.VMEM((2, tokens, q_latent.shape[1]), bf16),
            pltpu.VMEM((3, kv_latent.shape[1], tokens), bf16),
            pltpu.VMEM((2, ctx * q_weight.shape[0], wide_q), bf16),
            pltpu.VMEM((2, ctx * kv_weight.shape[0], wide_kv), bf16),
            pltpu.VMEM((2, columns, out_weight.shape[0]), bf16),
            pltpu.VMEM((1, documents.shape[0] + tokens), f32),
            pltpu.VMEM((3 * tokens, 128), f32),
            pltpu.VMEM((2, tokens, 2 * tokens), f32),
            pltpu.VMEM((3 * tokens, KL), bf16),
            pltpu.VMEM((3 * tokens, ROPE), bf16),
            pltpu.VMEM((2 * tokens, wide_q), f32),
            pltpu.VMEM((3 * tokens, wide_kv), bf16),
            pltpu.VMEM((2, 2, tokens, depth), bf16),
            pltpu.VMEM((2, Z, 2, tokens, depth), bf16),
            pltpu.VMEM((2, tokens, columns), f32),
            pltpu.VMEM((Z, tokens, columns), bf16),
            pltpu.VMEM((Z, tokens, columns), bf16),
            pltpu.VMEM((Z, tokens, columns), bf16),
            pltpu.VMEM((Z, Z - 1, part, columns), bf16),
            pltpu.VMEM((Z, part, columns), bf16),
            pltpu.VMEM((Z, part, columns), bf16),
            pltpu.VMEM((tokens, columns), bf16),
            pltpu.SemaphoreType.DMA((112,)),
            pltpu.SemaphoreType.DMA((112,)),
            pltpu.SemaphoreType.DMA((7,)),
            pltpu.SemaphoreType.DMA((Z,)),
            pltpu.SemaphoreType.DMA((Z,)),
            pltpu.SemaphoreType.DMA((Z,)),
            pltpu.SemaphoreType.DMA((Z,)),
            pltpu.SemaphoreType.DMA((2,)),
        ],
        compiler_params=pltpu.CompilerParams(
            collective_id=0, has_side_effects=True, vmem_limit_bytes=50 << 20
        ),
        name="layer",
    )(
        q_latent,
        kv_latent.T,
        q_weight,
        kv_weight,
        out_weight.T,
        kv_gain[None, :],
        inverse,
        documents[None, :],
    )


def solution(mesh):
    return jax.shard_map(
        per_device,
        mesh=mesh,
        in_specs=(
            P("ctx", None),
            P("ctx", None),
            P(),
            P("ctx", "grp"),
            P("ctx", "grp"),
            P("grp", "ctx"),
            P(),
        ),
        out_specs=P("ctx", "grp"),
        check_vma=False,
    )
```

time: 126 us -> 126 us (level)
  local copies, waits for them, and re-layouts: 1.94 us -> 7.34 us
  Pallas kernels: 122 us -> 118 us
  other arithmetic: 1.84 us -> 0.02 us
    unnamed x12 -> x14, local copies, waits for them, and re-layouts: 0.03 us -> 6.51 us
    pallas_call x3 -> x1, Pallas kernels: 122 us -> 118 us  [per_device(): pl.pallas_call(layer_kernel, out_shape=jax.ShapeDtypeStruct((tokens, colu...]
    cos x1 -> x0, other arithmetic: 1.45 us -> none  [per_device(): cosine, sine = (jnp.cos(angles), jnp.sin(angles))]
where the time goes in v4:
time: 126 us
  Pallas kernels  118 us (94%)
  local copies, waits for them, and re-layouts  7.34 us (6%)
    pallas_call x1, Pallas kernels, per_device(): pl.pallas_call(layer_kernel, out_shape=jax.ShapeDtypeStruct((tokens, colu...  118 us
    unnamed x14, local copies, waits for them, and re-layouts  6.51 us

profile of v4, /device:TPU:8, one launch (start us, length us, event | category | flops | bytes accessed | tf_op | source)
XLA Modules:
  0.0 125.8 jit_solution(7287356963502182574)
XLA Ops:
  0.0 0.0 copy-start.6
  0.0 0.7 copy-done.6
  0.7 0.0 copy-start
  0.7 1.2 copy-done
  1.9 0.0 copy-start.1
  1.9 1.1 copy-done.1
  3.0 0.0 copy-start.2
  3.0 1.0 copy-done.2
  4.0 0.0 copy-start.3
  4.0 1.0 copy-done.3
  4.9 0.0 copy-start.4
  4.9 0.9 copy-done.4
  5.8 0.0 copy-start.5
  5.8 0.7 copy-done.5
  6.5 118.4 %layer.1 = bf16[256,448]{1,0:T(8,128)(2,1)S(1)} custom-call(bf16[256,1536]{1,0:T(8,128)(2,1)S(1)} %copy-done.1, bf16[576,256]{1,0:T(8,128)(2,1)S(1)} %bitcast.5, bf16[96,1536]{1,0:T(8,128)(2,1)S(1)} %copy-done.3, bf16[32,2048]{1,0:T(8,128)(2,1)S(1)} %copy-done.4, bf16[448,1024]{1,0:T(8,128)(2,1)S(1)} %bitcast.4, f32[1,512]{1,0:T(1,128)S(1)} %bitcast.7, ...), custom_call_target="tpu_custom_call" | custom-call | tf_op jit(solution)/shard_map/layer/pallas_call | solution.py:509
  125.0 0.8 copy.8
  (1 shorter events, 0.0 us)
Async XLA Ops:
  0.0 0.7 copy-start.6
  0.7 1.2 copy-start
  1.9 1.1 copy-start.1
  3.0 1.0 copy-start.2
  4.0 1.0 copy-start.3
  4.9 0.9 copy-start.4
  5.8 0.7 copy-start.5

commit v5 on v4

--- a/solution.py
+++ b/solution.py
@@ -13,6 +13,7 @@
 Z = 8
 MESH = pl.DeviceIdType.MESH
 VM = pl.BlockSpec(memory_space=pltpu.VMEM)
+HBM = pl.BlockSpec(memory_space=pltpu.HBM)
 EPSILON = 1e-06
 OFFSETS = [0, 7, 1, 6, 2, 5, 3, 4]
 
@@ -40,33 +41,34 @@
         self.send_sems = send_sems
         self.recv_sems = recv_sems
         self.used = 0
-        self.started = []
+        self.groups = 0
 
     def slot(self):
         self.used += 1
         return self.used - 1
 
-    def make(self, number, source, target, device):
+    def group(self):
+        self.groups += 1
+        return self.groups - 1
+
+    def make(self, group, number, source, target, device):
         return pltpu.make_async_remote_copy(
             source,
             target,
-            self.send_sems.at[number],
+            self.send_sems.at[group],
             self.recv_sems.at[number],
             device_id=device,
             device_id_type=MESH,
         )
 
-    def start(self, number, source, target, device):
-        copy = self.make(number, source, target, device)
-        copy.start()
-        self.started.append(copy)
+    def start(self, group, number, source, target, device):
+        self.make(group, number, source, target, device).start()
 
     def arrived(self, number, target, device):
-        self.make(number, target, target, device).wait_recv()
-
-    def drain(self):
-        for copy in self.started:
-            copy.wait_send()
+        self.make(0, number, target, target, device).wait_recv()
+
+    def sent(self, group, volume, device):
+        self.make(group, 0, volume, volume, device).wait_send()
 
 
 def enter(devices):
@@ -77,8 +79,9 @@
 
 
 class Ring:
-    def __init__(self, sends, place, views):
+    def __init__(self, sends, place, views, groups):
         self.sends = sends
+        self.groups = groups
         self.place = place
         self.views = views
         self.up = place.at(z=(place.z + 1) % Z)
@@ -101,6 +104,7 @@
         targets = self.views(origin, part)
         for which, (source, target) in enumerate(zip(sources or targets, targets)):
             self.sends.start(
+                self.groups[which],
                 self.number(way, steps, part, which),
                 source,
                 target,
@@ -133,15 +137,19 @@
 
 
 def layer_kernel(
-    ql,
-    kvl,
+    ql_in,
+    kvl_in,
+    qw_in,
+    kvw_in,
+    ow_in,
+    gain_in,
+    documents_in,
+    inverse,
+    out,
     qw,
     kvw,
-    ow,
     gain,
-    inverse,
     documents,
-    out,
     all_ql,
     all_kvl,
     all_qw,
@@ -167,6 +175,7 @@
     send_sems,
     recv_sems,
     local_sems,
+    own_sems,
     part_send,
     part_recv,
     move_send,
@@ -180,9 +189,26 @@
     fellows = [me.at(chip=(me.chip + step) % Z) for step in range(1, Z)]
     column = [me.at(z=(me.z + step) % Z) for step in range(1, Z)]
     above = column[0]
+    local = []
+    for number, (source, target) in enumerate(
+        [
+            (qw_in, qw),
+            (kvw_in, kvw),
+            (kvl_in, all_kvl.at[1 + me.y]),
+            (ql_in, all_ql.at[me.y]),
+            (documents_in, documents),
+            (gain_in, gain),
+            (ow_in, all_ow.at[me.y]),
+        ]
+    ):
+        copy = pltpu.make_async_copy(source, target, local_sems.at[number])
+        copy.start()
+        local.append(copy)
     enter([peer, twin] + fellows + column)
+    for number in (0, 1):
+        local[number].wait()
     sends = Sends(send_sems, recv_sems)
-    tokens = ql.shape[0]
+    tokens = ql_in.shape[0]
     deep_q, deep_kv = qw.shape[0], kvw.shape[0]
     wide_q, wide_kv = qw.shape[1] // 4, kvw.shape[1] // 4
     depth = att.shape[3]
@@ -217,8 +243,13 @@
 
         return views
 
-    weights = [Ring(sends, me, weight_views(pair)) for pair in range(2)]
-    results = [Ring(sends, me, attended_views(pair)) for pair in range(2)]
+    weights = [
+        Ring(sends, me, weight_views(pair), [sends.group(), sends.group()]) for pair in range(2)
+    ]
+    results = [Ring(sends, me, attended_views(pair), [sends.group()]) for pair in range(2)]
+    back_groups = [sends.group() for _ in range(2)]
+    twin_group, prior_group, lat_q_group, lat_kv_group = (sends.group() for _ in range(4))
+    twin_q_group, twin_kv_group, twin_prior_group, out_group = (sends.group() for _ in range(4))
     swaps = [[sends.slot(), sends.slot()] for _ in range(2)]
     backs = [sends.slot() for _ in range(2)]
     twins = [sends.slot() for _ in range(Z)]
@@ -232,21 +263,50 @@
         ring.send(0, 1, part, sources)
         ring.send(1, 1, part, sources)
 
+    def start_weights(pair, part):
+        ring = weights[pair]
+        if part == 0:
+            begin(ring, 0, cut(me.y, pair))
+            for number, (source, target) in enumerate(
+                zip(cut(me.y, pair), ring.views(me.z, 0))
+            ):
+                copy = pltpu.make_async_copy(source, target, own_sems.at[2 * pair + number])
+                copy.start()
+                own.append(copy)
+        else:
+            for number, target in zip(swaps[pair], ring.views(me.z, 1)):
+                sends.arrived(number, target, peer)
+            begin(ring, 1, None)
+
     def swap_weights(pair):
-        for number, source, target in zip(
-            swaps[pair], cut(1 - me.y, pair), weights[pair].views(me.z, 0)
+        for group, number, source, target in zip(
+            weights[pair].groups, swaps[pair], cut(1 - me.y, pair), weights[pair].views(me.z, 0)
         ):
-            sends.start(number, source, target, peer)
-
-    def swapped_weights(pair):
-        for number, target in zip(swaps[pair], weights[pair].views(me.z, 1)):
-            sends.arrived(number, target, peer)
-
+            sends.start(group, number, source, target, peer)
+
+    def start_results(pair, part):
+        ring = results[pair]
+        if part == 0:
+            sends.start(
+                back_groups[pair],
+                backs[pair],
+                att.at[pair, 1 - me.y],
+                every.at[pair, me.z, me.y],
+                peer,
+            )
+            begin(ring, 0, [att.at[pair, me.y]])
+        else:
+            sends.arrived(backs[pair], every.at[pair, me.z, 1 - me.y], peer)
+            begin(ring, 1, None)
+
+    own = []
     half = tokens // 2
     near = pl.ds(pl.multiple_of(me.core * half, half), half)
     far = pl.ds(pl.multiple_of((1 - me.core) * half, half), half)
 
     def make_tables():
+        local[4].wait()
+        local[5].wait()
         docs[:, :tokens] = jnp.full((1, tokens), -1.0, jnp.float32)
         docs[:, tokens:] = documents[...].astype(jnp.float32)
         key_docs = docs[:, pl.ds(pl.multiple_of(me.z * 2 * tokens, 128), 3 * tokens)]
@@ -269,7 +329,42 @@
             lane < ROPE, jnp.cos(angles), jnp.where(lane < ROPE + ROPE // 2, -sine, sine)
         )
 
+    def send_latent_kv():
+        local[2].wait()
+        block = all_kvl.at[1 + me.y, :, near]
+        sends.start(lat_kv_group, lat_kv, block, block, peer)
+
+    def send_latent_q():
+        local[3].wait()
+        block = all_ql.at[me.y, near]
+        sends.start(lat_q_group, lat_q, block, block, peer)
+
+    def send_out():
+        local[6].wait()
+        block = all_ow.at[me.y]
+        sends.start(out_group, swap_out, block, block, peer)
+
+    def send_prior():
+        block = all_kvl.at[2 - me.y, :, near]
+        sends.arrived(lat_kv, block, peer)
+        sends.start(
+            prior_group, prior, all_kvl.at[2, :, near], all_kvl.at[0, :, near], above
+        )
+        sends.start(twin_kv_group, twin_kv, block, block, twin)
+
+    def pass_latent_q():
+        block = all_ql.at[1 - me.y, near]
+        sends.arrived(lat_q, block, peer)
+        sends.start(twin_q_group, twin_q, block, block, twin)
+
+    def pass_prior():
+        block = all_kvl.at[0, :, near]
+        sends.arrived(prior, block, above)
+        sends.start(twin_prior_group, twin_prior, block, block, twin)
+
     def make_keys():
+        sends.arrived(twin_kv, all_kvl.at[2 - me.y, :, far], twin)
+        sends.arrived(twin_prior, all_kvl.at[0, :, far], twin)
         latents = jnp.concatenate(
             [all_kvl[number].astype(jnp.float32).T for number in range(3)], axis=0
         )
@@ -279,6 +374,10 @@
         key_rope[...] = turn(latents[:, KL:], table[...]).astype(bf16)
 
     def make_pair(pair):
+        if pair == 0:
+            sends.arrived(twin_q, all_ql.at[1 - me.y, far], twin)
+        for copy in own[2 * pair : 2 * pair + 2]:
+            copy.wait()
         for block in range(2):
             query[tokens * block : tokens * (block + 1), :] = dot(all_ql[block], all_qw[pair])
         key_value[...] = dot(normed[...], all_kvw[pair]).astype(bf16)
@@ -299,12 +398,6 @@
             mixed = dot(powers.astype(bf16), values[window]) * (1.0 / total)
             att[pair, block, :, head * VDIM : (head + 1) * VDIM] = mixed.astype(bf16)
 
-    def swap_attended(pair):
-        sends.start(backs[pair], att.at[pair, 1 - me.y], every.at[pair, me.z, me.y], peer)
-
-    def swapped_attended(pair):
-        sends.arrived(backs[pair], every.at[pair, me.z, 1 - me.y], peer)
-
     def product(number, z, which):
         total = None
         for y in (me.y, 1 - me.y):
@@ -320,34 +413,36 @@
 
     def tile(number):
         z = (me.z + OFFSETS[number]) % Z
+        if number == 0:
+            sends.arrived(swap_out, all_ow.at[1 - me.y], peer)
         given[number] = product(number, z, 1 - me.core).astype(bf16)
-        sends.start(twins[number], given.at[number], taken.at[number], twin)
-        kept[number % 2] = product(number, z, me.core)
+        sends.start(twin_group, twins[number], given.at[number], taken.at[number], twin)
+        kept[number] = product(number, z, me.core)
 
     def spread(number):
         sends.arrived(twins[number], taken.at[number], twin)
-        summed[number] = (kept[number % 2] + taken[number].astype(jnp.float32)).astype(bf16)
+        summed[number] = (kept[number] + taken[number].astype(jnp.float32)).astype(bf16)
         for step in range(1, Z):
             chip = (me.chip + step) % Z
             part = pl.ds(pl.multiple_of(chip * rows, rows), rows)
             remote(
                 summed.at[number, part],
                 inbox.at[number, step - 1],
-                part_send.at[number],
+                part_send.at[0],
                 part_recv.at[number],
                 fellows[step - 1],
             ).start()
 
     def parts(number):
         return remote(
-            inbox.at[number], inbox.at[number], part_send.at[number], part_recv.at[number], peer
+            inbox.at[number], inbox.at[number], part_send.at[0], part_recv.at[number], peer
         )
 
     def move(number):
         return remote(
             reduced.at[number],
             moved.at[number],
-            move_send.at[number],
+            move_send.at[0],
             move_recv.at[number],
             me.at(z=(me.z + OFFSETS[number]) % Z),
         )
@@ -379,118 +474,137 @@
             ).start()
 
     swap_weights(0)
-    begin(weights[0], 0, cut(me.y, 0))
-    local = []
-    for source, target in [
-        (cut(me.y, 0)[0], weights[0].views(me.z, 0)[0]),
-        (cut(me.y, 0)[1], weights[0].views(me.z, 0)[1]),
-        (cut(me.y, 1)[0], weights[1].views(me.z, 0)[0]),
-        (cut(me.y, 1)[1], weights[1].views(me.z, 0)[1]),
-        (kvl, all_kvl.at[1 + me.y]),
-        (ql, all_ql.at[me.y]),
-        (ow, all_ow.at[me.y]),
-    ]:
-        copy = pltpu.make_async_copy(source, target, local_sems.at[len(local)])
-        copy.start()
-        local.append(copy)
-    sends.start(lat_kv, kvl.at[:, near], all_kvl.at[1 + me.y, :, near], peer)
-    sends.start(lat_q, ql.at[near], all_ql.at[me.y, near], peer)
-    swapped_weights(0)
-    begin(weights[0], 1, None)
+    start_weights(0, 0)
+    send_latent_kv()
     swap_weights(1)
+    send_latent_q()
+    start_weights(1, 0)
+    start_weights(0, 1)
+    weights[0].arrive(1, 1, 0)
+    weights[0].arrive(0, 1, 0)
+    send_prior()
+    weights[0].arrive(1, 1, 1)
+    send_out()
+    weights[0].arrive(0, 2, 0)
+    start_weights(1, 1)
+    weights[0].arrive(1, 2, 0)
     make_tables()
-    both(weights[0], 1, 0)
-    sends.start(swap_out, ow, all_ow.at[me.y], peer)
-    local[4].wait()
-    sends.arrived(lat_kv, all_kvl.at[2 - me.y, :, near], peer)
-    sends.start(prior, all_kvl.at[2, :, near], all_kvl.at[0, :, near], above)
-    sends.start(
-        twin_kv, all_kvl.at[2 - me.y, :, near], all_kvl.at[2 - me.y, :, near], twin
-    )
-    both(weights[0], 1, 1)
-    sends.arrived(lat_q, all_ql.at[1 - me.y, near], peer)
-    sends.start(twin_q, all_ql.at[1 - me.y, near], all_ql.at[1 - me.y, near], twin)
-    both(weights[0], 2, 0)
-    sends.arrived(prior, all_kvl.at[0, :, near], above)
-    sends.start(twin_prior, all_kvl.at[0, :, near], all_kvl.at[0, :, near], twin)
-    both(weights[0], 2, 1)
-    both(weights[0], 3, 0)
-    both(weights[0], 3, 1)
-    begin(weights[1], 0, cut(me.y, 1))
-    swapped_weights(1)
-    begin(weights[1], 1, None)
-    sends.arrived(twin_kv, all_kvl.at[2 - me.y, :, far], twin)
-    sends.arrived(twin_prior, all_kvl.at[0, :, far], twin)
+    weights[0].arrive(0, 1, 1)
+    weights[0].arrive(1, 2, 1)
+    weights[1].arrive(1, 1, 0)
+    pass_latent_q()
+    weights[1].arrive(0, 1, 0)
+    weights[0].arrive(0, 3, 0)
+    weights[1].arrive(1, 1, 1)
+    weights[0].arrive(0, 2, 1)
+    weights[1].arrive(0, 2, 0)
+    weights[0].arrive(1, 3, 1)
+    pass_prior()
+    weights[1].arrive(0, 1, 1)
+    weights[0].arrive(0, 4, 0)
+    weights[1].arrive(1, 2, 1)
     make_keys()
-    both(weights[0], 4, 0)
-    both(weights[0], 4, 1)
-    sends.arrived(twin_q, all_ql.at[1 - me.y, far], twin)
-    for number in (0, 1, 5):
-        local[number].wait()
+    weights[0].arrive(1, 3, 0)
+    weights[1].arrive(1, 2, 0)
+    weights[0].arrive(0, 3, 1)
+    weights[0].arrive(1, 4, 1)
     make_pair(0)
-    both(weights[1], 1, 0)
-    both(weights[1], 1, 1)
+    weights[1].arrive(0, 3, 0)
     attend(0, 0)
-    both(weights[1], 2, 0)
+    weights[1].arrive(1, 3, 1)
     attend(0, 1)
-    swap_attended(0)
-    begin(results[0], 0, [att.at[0, me.y]])
-    both(weights[1], 2, 1)
-    both(weights[1], 3, 0)
-    both(weights[1], 3, 1)
-    swapped_attended(0)
-    begin(results[0], 1, None)
-    both(weights[1], 4, 0)
-    both(weights[1], 4, 1)
-    for number in (2, 3):
-        local[number].wait()
+    weights[1].arrive(0, 2, 1)
+    start_results(0, 0)
+    weights[1].arrive(0, 4, 0)
+    weights[1].arrive(1, 4, 1)
+    weights[1].arrive(1, 3, 0)
+    weights[1].arrive(0, 3, 1)
     make_pair(1)
-    both(results[0], 1, 0)
+    start_results(0, 1)
     attend(1, 0)
-    both(results[0], 1, 1)
     attend(1, 1)
-    swap_attended(1)
-    begin(results[1], 0, [att.at[1, me.y]])
-    both(results[0], 2, 0)
-    both(results[0], 2, 1)
-    swapped_attended(1)
-    begin(results[1], 1, None)
-    local[6].wait()
-    sends.arrived(swap_out, all_ow.at[1 - me.y], peer)
+    start_results(1, 0)
+    results[0].arrive(0, 1, 0)
+    start_results(1, 1)
+    results[1].arrive(1, 1, 0)
+    results[1].arrive(0, 1, 0)
     tile(0)
-    for steps in range(1, 4):
-        for part in (0, 1):
-            if steps == 1:
-                both(results[0], 3, part)
-            both(results[1], steps, part)
-            if steps == 2:
-                both(results[0], 4, part)
-        for number in (2 * steps - 1, 2 * steps):
-            spread(number - 1)
-            tile(number)
-            if number >= 3:
-                finish(number - 3)
+    results[0].arrive(1, 1, 0)
+    results[0].arrive(0, 1, 1)
+    results[1].arrive(1, 1, 1)
+    results[0].arrive(1, 1, 1)
+    spread(0)
+    results[1].arrive(0, 1, 1)
+    tile(2)
+    spread(2)
+    results[0].arrive(1, 2, 0)
+    results[0].arrive(0, 2, 0)
+    tile(1)
+    results[1].arrive(1, 2, 1)
+    results[0].arrive(0, 2, 1)
+    results[1].arrive(0, 2, 0)
+    spread(1)
+    results[1].arrive(0, 2, 1)
+    results[0].arrive(1, 2, 1)
+    results[1].arrive(1, 2, 0)
+    tile(4)
+    spread(4)
+    tile(3)
+    results[1].arrive(0, 3, 0)
+    spread(3)
+    results[0].arrive(0, 3, 1)
+    results[0].arrive(0, 3, 0)
+    results[1].arrive(1, 3, 1)
+    results[0].arrive(1, 3, 0)
+    results[0].arrive(1, 3, 1)
+    results[1].arrive(0, 3, 1)
+    tile(5)
+    finish(4)
+    spread(5)
+    results[1].arrive(1, 3, 0)
+    tile(6)
+    finish(1)
+    results[1].arrive(0, 4, 0)
     spread(6)
-    finish(4)
-    for number in range(3):
-        deliver(number)
-    both(results[1], 4, 0)
-    both(results[1], 4, 1)
+    finish(2)
+    results[0].arrive(0, 4, 0)
+    results[1].arrive(1, 4, 1)
+    results[0].arrive(1, 4, 1)
     tile(7)
-    finish(5)
+    finish(0)
     spread(7)
     finish(6)
+    deliver(0)
+    finish(3)
+    finish(5)
+    deliver(1)
+    deliver(4)
+    deliver(2)
+    finish(7)
     deliver(3)
-    deliver(4)
-    finish(7)
+    deliver(6)
     deliver(5)
-    deliver(6)
     deliver(7)
-    sends.drain()
-    for number in range(Z):
-        parts(number).wait_send()
-        if number:
-            move(number).wait_send()
+    for pair in range(2):
+        group_q, group_kv = weights[pair].groups
+        sends.sent(group_q, all_qw.at[pair, pl.ds(0, 15 * deep_q)], peer)
+        sends.sent(group_kv, all_kvw.at[pair, pl.ds(0, 15 * deep_kv)], peer)
+        sends.sent(results[pair].groups[0], every.at[pair, pl.ds(0, 7)], peer)
+        sends.sent(back_groups[pair], att.at[pair, 0], peer)
+    sends.sent(twin_group, given, peer)
+    for group, volume in [
+        (prior_group, all_kvl.at[0, :, near]),
+        (lat_q_group, all_ql.at[0, near]),
+        (lat_kv_group, all_kvl.at[0, :, near]),
+        (twin_q_group, all_ql.at[0, near]),
+        (twin_kv_group, all_kvl.at[0, :, near]),
+        (twin_prior_group, all_kvl.at[0, :, near]),
+        (out_group, all_ow.at[0]),
+    ]:
+        sends.sent(group, volume, peer)
+    remote(inbox, inbox, part_send.at[0], part_recv.at[0], peer).wait_send()
+    moves = moved.at[pl.ds(0, Z - 1)]
+    remote(moves, moves, move_send.at[0], move_recv.at[0], peer).wait_send()
     everyone = final.at[pl.ds(0, rows * (Z - 1))]
     remote(everyone, everyone, last.at[0], last.at[1], peer).wait()
     out[...] = final[...]
@@ -509,9 +623,13 @@
     return pl.pallas_call(
         layer_kernel,
         out_shape=jax.ShapeDtypeStruct((tokens, columns), bf16),
-        in_specs=[VM] * 8,
+        in_specs=[HBM] * 7 + [VM],
         out_specs=VM,
         scratch_shapes=[
+            pltpu.VMEM(q_weight.shape, bf16),
+            pltpu.VMEM(kv_weight.shape, bf16),
+            pltpu.VMEM((1, kv_gain.shape[0]), f32),
+            pltpu.VMEM((1, documents.shape[0]), jnp.int32),
             pltpu.VMEM((2, tokens, q_latent.shape[1]), bf16),
             pltpu.VMEM((3, kv_latent.shape[1], tokens), bf16),
             pltpu.VMEM((2, ctx * q_weight.shape[0], wide_q), bf16),
@@ -526,7 +644,7 @@
             pltpu.VMEM((3 * tokens, wide_kv), bf16),
             pltpu.VMEM((2, 2, tokens, depth), bf16),
             pltpu.VMEM((2, Z, 2, tokens, depth), bf16),
-            pltpu.VMEM((2, tokens, columns), f32),
+            pltpu.VMEM((Z, tokens, columns), f32),
             pltpu.VMEM((Z, tokens, columns), bf16),
             pltpu.VMEM((Z, tokens, columns), bf16),
             pltpu.VMEM((Z, tokens, columns), bf16),
@@ -534,17 +652,18 @@
             pltpu.VMEM((Z, part, columns), bf16),
             pltpu.VMEM((Z, part, columns), bf16),
             pltpu.VMEM((tokens, columns), bf16),
-            pltpu.SemaphoreType.DMA((112,)),
-            pltpu.SemaphoreType.DMA((112,)),
+            pltpu.SemaphoreType.DMA((16,)),
+            pltpu.SemaphoreType.DMA((105,)),
             pltpu.SemaphoreType.DMA((7,)),
+            pltpu.SemaphoreType.DMA((4,)),
+            pltpu.SemaphoreType.DMA((1,)),
             pltpu.SemaphoreType.DMA((Z,)),
-            pltpu.SemaphoreType.DMA((Z,)),
-            pltpu.SemaphoreType.DMA((Z,)),
+            pltpu.SemaphoreType.DMA((1,)),
             pltpu.SemaphoreType.DMA((Z,)),
             pltpu.SemaphoreType.DMA((2,)),
         ],
         compiler_params=pltpu.CompilerParams(
-            collective_id=0, has_side_effects=True, vmem_limit_bytes=50 << 20
+            collective_id=0, has_side_effects=True, vmem_limit_bytes=127 << 19
         ),
         name="layer",
     )(
@@ -554,8 +673,8 @@
         kv_weight,
         out_weight.T,
         kv_gain[None, :],
+        documents[None, :],
         inverse,
-        documents[None, :],
     )
 
 

time: 126 us -> 111 us (0.88)
  Pallas kernels: 118 us -> 108 us
  local copies, waits for them, and re-layouts: 7.34 us -> 1.78 us
    pallas_call x1, Pallas kernels: 118 us -> 108 us  [per_device(): pl.pallas_call(layer_kernel, out_shape=jax.ShapeDtypeStruct((tokens, colu...]
    unnamed x14 -> x0, local copies, waits for them, and re-layouts: 6.51 us -> none
where the time goes in v5:
time: 111 us; the launch traced here: 110 us
  Pallas kernels  108 us (97%)
  local copies, waits for them, and re-layouts  1.78 us (2%)
    pallas_call x1, Pallas kernels, per_device(): pl.pallas_call(layer_kernel, out_shape=jax.ShapeDtypeStruct((tokens, colu...  108 us

profile of v5, /device:TPU:8, one launch (start us, length us, event | category | flops | bytes accessed | tf_op | source)
XLA Modules:
  0.0 110.4 jit_solution(2835026502756073164)
XLA Ops:
  0.0 0.5 fusion.1.inverse
  0.5 108.0 %layer.1 = bf16[256,448]{1,0:T(8,128)(2,1)} custom-call(bf16[256,1536]{1,0:T(8,128)(2,1)} %ql_in.1, bf16[576,256]{1,0:T(8,128)(2,1)} %bitcast.5, bf16[96,1536]{1,0:T(8,128)(2,1)} %qw_in.1, bf16[32,2048]{1,0:T(8,128)(2,1)} %kvw_in.1, bf16[448,1024]{1,0:T(8,128)(2,1)} %bitcast.4, f32[1,512]{1,0:T(1,128)} %bitcast.7, s32[1,4096]{1,0:T(1,128)} %bitcast.6, ...), custom_call_target="tpu_custom_call" | custom-call | tf_op jit(solution)/shard_map/layer/pallas_call | solution.py:623
  108.6 1.8 %copy.8 = bf16[256,448]{0,1:T(8,128)(2,1)} copy(bf16[256,448]{1,0:T(8,128)(2,1)} %layer.1) | data formatting | bytes 458752 | tf_op jit(solution)/shard_map/layer/pallas_call | solution.py:623

commit v6 on v5

--- a/solution.py
+++ b/solution.py
@@ -172,6 +172,7 @@
     reduced,
     moved,
     final,
+    ahead,
     send_sems,
     recv_sems,
     local_sems,
@@ -187,8 +188,8 @@
     peer = me.at(y=1 - me.y)
     twin = me.at(core=1 - me.core)
     fellows = [me.at(chip=(me.chip + step) % Z) for step in range(1, Z)]
-    column = [me.at(z=(me.z + step) % Z) for step in range(1, Z)]
-    above = column[0]
+    above = me.at(z=(me.z + 1) % Z)
+    below = me.at(z=(me.z + Z - 1) % Z)
     local = []
     for number, (source, target) in enumerate(
         [
@@ -204,7 +205,7 @@
         copy = pltpu.make_async_copy(source, target, local_sems.at[number])
         copy.start()
         local.append(copy)
-    enter([peer, twin] + fellows + column)
+    enter([peer, twin, above, below] + fellows)
     for number in (0, 1):
         local[number].wait()
     sends = Sends(send_sems, recv_sems)
@@ -398,10 +399,10 @@
             mixed = dot(powers.astype(bf16), values[window]) * (1.0 / total)
             att[pair, block, :, head * VDIM : (head + 1) * VDIM] = mixed.astype(bf16)
 
-    def product(number, z, which):
+    def product(number, z, which, pairs=(0, 1)):
         total = None
         for y in (me.y, 1 - me.y):
-            for pair in range(2):
+            for pair in pairs:
                 if number == 0 and y is me.y:
                     left = att[pair, y]
                 else:
@@ -415,9 +416,21 @@
         z = (me.z + OFFSETS[number]) % Z
         if number == 0:
             sends.arrived(swap_out, all_ow.at[1 - me.y], peer)
-        given[number] = product(number, z, 1 - me.core).astype(bf16)
+        if number == Z - 1:
+            ahead[...] = ahead[...] + product(number, z, 1 - me.core, (1,))
+            given[number] = ahead[...].astype(bf16)
+        else:
+            given[number] = product(number, z, 1 - me.core).astype(bf16)
         sends.start(twin_group, twins[number], given.at[number], taken.at[number], twin)
-        kept[number] = product(number, z, me.core)
+        if number == Z - 1:
+            kept[number] = kept[number] + product(number, z, me.core, (1,))
+        else:
+            kept[number] = product(number, z, me.core)
+
+    def tile_ahead():
+        z = (me.z + OFFSETS[Z - 1]) % Z
+        ahead[...] = product(Z - 1, z, 1 - me.core, (0,))
+        kept[Z - 1] = product(Z - 1, z, me.core, (0,))
 
     def spread(number):
         sends.arrived(twins[number], taken.at[number], twin)
@@ -447,6 +460,15 @@
             me.at(z=(me.z + OFFSETS[number]) % Z),
         )
 
+    def direct():
+        return remote(
+            reduced.at[Z - 1],
+            final.at[mine],
+            last.at[0],
+            last.at[1],
+            me.at(z=(me.z + OFFSETS[Z - 1]) % Z, chip=me.z),
+        )
+
     def finish(number):
         parts(number).wait_recv()
         total = summed[number, mine, :].astype(jnp.float32)
@@ -456,7 +478,7 @@
             moved[0] = total.astype(bf16)
         else:
             reduced[number] = total.astype(bf16)
-            move(number).start()
+            (direct() if number == Z - 1 else move(number)).start()
 
     def deliver(number):
         if number:
@@ -564,12 +586,13 @@
     results[1].arrive(1, 3, 0)
     tile(6)
     finish(1)
-    results[1].arrive(0, 4, 0)
     spread(6)
     finish(2)
     results[0].arrive(0, 4, 0)
+    results[0].arrive(1, 4, 1)
+    tile_ahead()
+    results[1].arrive(0, 4, 0)
     results[1].arrive(1, 4, 1)
-    results[0].arrive(1, 4, 1)
     tile(7)
     finish(0)
     spread(7)
@@ -584,7 +607,6 @@
     deliver(3)
     deliver(6)
     deliver(5)
-    deliver(7)
     for pair in range(2):
         group_q, group_kv = weights[pair].groups
         sends.sent(group_q, all_qw.at[pair, pl.ds(0, 15 * deep_q)], peer)
@@ -603,10 +625,16 @@
     ]:
         sends.sent(group, volume, peer)
     remote(inbox, inbox, part_send.at[0], part_recv.at[0], peer).wait_send()
-    moves = moved.at[pl.ds(0, Z - 1)]
+    moves = moved.at[pl.ds(0, Z - 2)]
     remote(moves, moves, move_send.at[0], move_recv.at[0], peer).wait_send()
-    everyone = final.at[pl.ds(0, rows * (Z - 1))]
-    remote(everyone, everyone, last.at[0], last.at[1], peer).wait()
+    opposite = (me.z - me.chip + Z) % Z == OFFSETS[Z - 1]
+    for pick, count in ((opposite, Z), (jnp.logical_not(opposite), Z - 1)):
+
+        @pl.when(pick)
+        def _():
+            volume = final.at[pl.ds(0, rows * count)]
+            remote(volume, volume, last.at[0], last.at[1], peer).wait()
+
     out[...] = final[...]
 
 
@@ -652,6 +680,7 @@
             pltpu.VMEM((Z, part, columns), bf16),
             pltpu.VMEM((Z, part, columns), bf16),
             pltpu.VMEM((tokens, columns), bf16),
+            pltpu.VMEM((tokens, columns), f32),
             pltpu.SemaphoreType.DMA((16,)),
             pltpu.SemaphoreType.DMA((105,)),
             pltpu.SemaphoreType.DMA((7,)),

time: 111 us -> 108 us (0.973)
  Pallas kernels: 108 us -> 105 us
    pallas_call x1, Pallas kernels: 108 us -> 105 us  [per_device(): pl.pallas_call(layer_kernel, out_shape=jax.ShapeDtypeStruct((tokens, colu...]
where the time goes in v6:
time: 108 us; the launch traced here: 107 us
  Pallas kernels  105 us (97%)
  local copies, waits for them, and re-layouts  1.78 us (2%)
    pallas_call x1, Pallas kernels, per_device(): pl.pallas_call(layer_kernel, out_shape=jax.ShapeDtypeStruct((tokens, colu...  105 us

profile of v6, /device:TPU:8, one launch (start us, length us, event | category | flops | bytes accessed | tf_op | source)
XLA Modules:
  0.0 107.4 jit_solution(15785653825784680155)
XLA Ops:
  0.0 0.5 fusion.1.inverse
  0.5 105.1 %layer.1 = bf16[256,448]{1,0:T(8,128)(2,1)} custom-call(bf16[256,1536]{1,0:T(8,128)(2,1)} %ql_in.1, bf16[576,256]{1,0:T(8,128)(2,1)} %bitcast.5, bf16[96,1536]{1,0:T(8,128)(2,1)} %qw_in.1, bf16[32,2048]{1,0:T(8,128)(2,1)} %kvw_in.1, bf16[448,1024]{1,0:T(8,128)(2,1)} %bitcast.4, f32[1,512]{1,0:T(1,128)} %bitcast.7, s32[1,4096]{1,0:T(1,128)} %bitcast.6, ...), custom_call_target="tpu_custom_call" | custom-call | tf_op jit(solution)/shard_map/layer/pallas_call | solution.py:651
  105.6 1.8 %copy.8 = bf16[256,448]{0,1:T(8,128)(2,1)} copy(bf16[256,448]{1,0:T(8,128)(2,1)} %layer.1) | data formatting | bytes 458752 | tf_op jit(solution)/shard_map/layer/pallas_call | solution.py:651

commit v7 on v6

--- a/solution.py
+++ b/solution.py
@@ -1,5 +1,6 @@
 import jax
 import jax.numpy as jnp
+import numpy as np
 from jax import lax
 from jax.experimental import pallas as pl
 from jax.experimental.pallas import tpu as pltpu
@@ -495,118 +496,118 @@
                 moved.at[number], final.at[mine], last.at[0], last.at[1], me.at(chip=chip)
             ).start()
 
+    start_weights(0, 0)
     swap_weights(0)
-    start_weights(0, 0)
+    start_weights(1, 0)
+    swap_weights(1)
     send_latent_kv()
-    swap_weights(1)
+    make_tables()
     send_latent_q()
-    start_weights(1, 0)
+    weights[0].arrive(0, 1, 0)
     start_weights(0, 1)
     weights[0].arrive(1, 1, 0)
-    weights[0].arrive(0, 1, 0)
+    weights[1].arrive(0, 1, 0)
+    start_weights(1, 1)
+    weights[0].arrive(0, 2, 0)
+    weights[0].arrive(1, 2, 0)
+    send_out()
+    weights[0].arrive(1, 1, 1)
+    weights[0].arrive(0, 1, 1)
     send_prior()
-    weights[0].arrive(1, 1, 1)
-    send_out()
-    weights[0].arrive(0, 2, 0)
-    start_weights(1, 1)
-    weights[0].arrive(1, 2, 0)
-    make_tables()
-    weights[0].arrive(0, 1, 1)
+    weights[1].arrive(1, 1, 1)
     weights[0].arrive(1, 2, 1)
+    weights[1].arrive(0, 1, 1)
     weights[1].arrive(1, 1, 0)
+    weights[0].arrive(0, 3, 0)
+    weights[1].arrive(0, 2, 0)
+    pass_prior()
     pass_latent_q()
-    weights[1].arrive(0, 1, 0)
-    weights[0].arrive(0, 3, 0)
-    weights[1].arrive(1, 1, 1)
-    weights[0].arrive(0, 2, 1)
-    weights[1].arrive(0, 2, 0)
-    weights[0].arrive(1, 3, 1)
-    pass_prior()
-    weights[1].arrive(0, 1, 1)
-    weights[0].arrive(0, 4, 0)
     weights[1].arrive(1, 2, 1)
     make_keys()
+    weights[0].arrive(1, 3, 1)
+    weights[1].arrive(1, 2, 0)
+    weights[0].arrive(0, 2, 1)
+    weights[1].arrive(1, 3, 1)
+    weights[1].arrive(0, 2, 1)
+    weights[0].arrive(0, 4, 0)
     weights[0].arrive(1, 3, 0)
-    weights[1].arrive(1, 2, 0)
+    weights[1].arrive(0, 3, 0)
+    weights[0].arrive(1, 4, 1)
     weights[0].arrive(0, 3, 1)
-    weights[0].arrive(1, 4, 1)
     make_pair(0)
-    weights[1].arrive(0, 3, 0)
     attend(0, 0)
-    weights[1].arrive(1, 3, 1)
+    weights[1].arrive(0, 3, 1)
     attend(0, 1)
-    weights[1].arrive(0, 2, 1)
+    weights[1].arrive(1, 3, 0)
+    weights[1].arrive(1, 4, 1)
     start_results(0, 0)
     weights[1].arrive(0, 4, 0)
-    weights[1].arrive(1, 4, 1)
-    weights[1].arrive(1, 3, 0)
-    weights[1].arrive(0, 3, 1)
     make_pair(1)
-    start_results(0, 1)
     attend(1, 0)
     attend(1, 1)
     start_results(1, 0)
+    results[0].arrive(1, 1, 0)
     results[0].arrive(0, 1, 0)
+    start_results(0, 1)
     start_results(1, 1)
+    tile(0)
     results[1].arrive(1, 1, 0)
+    results[0].arrive(0, 1, 1)
+    results[1].arrive(0, 1, 1)
+    results[0].arrive(1, 1, 1)
     results[1].arrive(0, 1, 0)
-    tile(0)
-    results[0].arrive(1, 1, 0)
-    results[0].arrive(0, 1, 1)
+    spread(0)
     results[1].arrive(1, 1, 1)
-    results[0].arrive(1, 1, 1)
-    spread(0)
-    results[1].arrive(0, 1, 1)
     tile(2)
+    results[1].arrive(1, 2, 0)
+    tile(1)
+    results[0].arrive(0, 2, 0)
     spread(2)
+    results[0].arrive(1, 2, 1)
     results[0].arrive(1, 2, 0)
-    results[0].arrive(0, 2, 0)
-    tile(1)
+    finish(0)
+    results[1].arrive(0, 2, 0)
     results[1].arrive(1, 2, 1)
     results[0].arrive(0, 2, 1)
-    results[1].arrive(0, 2, 0)
+    results[1].arrive(0, 2, 1)
     spread(1)
-    results[1].arrive(0, 2, 1)
-    results[0].arrive(1, 2, 1)
-    results[1].arrive(1, 2, 0)
     tile(4)
     spread(4)
+    results[1].arrive(1, 3, 0)
     tile(3)
+    results[0].arrive(0, 3, 1)
+    spread(3)
+    results[0].arrive(0, 3, 0)
     results[1].arrive(0, 3, 0)
-    spread(3)
-    results[0].arrive(0, 3, 1)
-    results[0].arrive(0, 3, 0)
+    results[0].arrive(1, 3, 1)
+    finish(1)
+    results[1].arrive(0, 3, 1)
+    tile(5)
     results[1].arrive(1, 3, 1)
     results[0].arrive(1, 3, 0)
-    results[0].arrive(1, 3, 1)
-    results[1].arrive(0, 3, 1)
-    tile(5)
+    spread(5)
+    tile(6)
+    finish(2)
+    results[0].arrive(1, 4, 1)
+    spread(6)
+    results[0].arrive(0, 4, 0)
     finish(4)
-    spread(5)
-    results[1].arrive(1, 3, 0)
-    tile(6)
-    finish(1)
-    spread(6)
-    finish(2)
-    results[0].arrive(0, 4, 0)
-    results[0].arrive(1, 4, 1)
+    results[1].arrive(0, 4, 0)
+    deliver(0)
     tile_ahead()
-    results[1].arrive(0, 4, 0)
     results[1].arrive(1, 4, 1)
     tile(7)
-    finish(0)
     spread(7)
-    finish(6)
-    deliver(0)
-    finish(3)
     finish(5)
     deliver(1)
-    deliver(4)
+    finish(6)
+    finish(3)
+    deliver(5)
     deliver(2)
     finish(7)
+    deliver(4)
+    deliver(6)
     deliver(3)
-    deliver(6)
-    deliver(5)
     for pair in range(2):
         group_q, group_kv = weights[pair].groups
         sends.sent(group_q, all_qw.at[pair, pl.ds(0, 15 * deep_q)], peer)
@@ -646,11 +647,11 @@
     depth = 2 * VDIM
     part = tokens // Z
     bf16, f32 = jnp.bfloat16, jnp.float32
-    spot = jnp.arange(128, dtype=f32) % (ROPE // 2)
-    inverse = (10000.0 ** (-2.0 * spot / ROPE))[None, :]
+    spot = np.arange(128) % (ROPE // 2)
+    inverse = (10000.0 ** (-2.0 * spot / ROPE)).astype(np.float32)[None, :]
     return pl.pallas_call(
         layer_kernel,
-        out_shape=jax.ShapeDtypeStruct((tokens, columns), bf16),
+        out_shape=pltpu.VMEM((tokens, columns), bf16),
         in_specs=[HBM] * 7 + [VM],
         out_specs=VM,
         scratch_shapes=[
@@ -692,7 +693,7 @@
             pltpu.SemaphoreType.DMA((2,)),
         ],
         compiler_params=pltpu.CompilerParams(
-            collective_id=0, has_side_effects=True, vmem_limit_bytes=127 << 19
+            collective_id=0, has_side_effects=True, vmem_limit_bytes=62 << 20
         ),
         name="layer",
     )(

time: 108 us -> 104 us (0.963)
  Pallas kernels: 105 us -> 103 us
    pallas_call x1, Pallas kernels: 105 us -> 103 us  [per_device(): pl.pallas_call(layer_kernel, out_shape=pltpu.VMEM((tokens, columns), bf16...]
where the time goes in v7:
time: 104 us; the launch traced here: 103 us
  Pallas kernels  103 us (99%)
    pallas_call x1, Pallas kernels, per_device(): pl.pallas_call(layer_kernel, out_shape=pltpu.VMEM((tokens, columns), bf16...  103 us

profile of v7, /device:TPU:8, one launch (start us, length us, event | category | flops | bytes accessed | tf_op | source)
XLA Modules:
  0.0 103.4 jit_solution(18049270871369653928)
XLA Ops:
  0.0 102.6 %layer.1 = bf16[256,448]{1,0:T(8,128)(2,1)S(1)} custom-call(bf16[256,1536]{1,0:T(8,128)(2,1)} %ql_in.1, bf16[576,256]{1,0:T(8,128)(2,1)} %bitcast.5, bf16[96,1536]{1,0:T(8,128)(2,1)} %qw_in.1, bf16[32,2048]{1,0:T(8,128)(2,1)} %kvw_in.1, bf16[448,1024]{1,0:T(8,128)(2,1)} %bitcast.4, f32[1,512]{1,0:T(1,128)} %bitcast.7, s32[1,4096]{1,0:T(1,128)} %bitcast.6, ...), custom_call_target="tpu_custom_call" | custom-call | tf_op jit(solution)/shard_map/layer/pallas_call | solution.py:652
  102.6 0.8 copy.9

commit v8 on v7

--- a/solution.py
+++ b/solution.py
@@ -602,9 +602,9 @@
     deliver(1)
     finish(6)
     finish(3)
+    finish(7)
     deliver(5)
     deliver(2)
-    finish(7)
     deliver(4)
     deliver(6)
     deliver(3)

time: 104 us -> 104 us (level)
  no operation moved by 1% of the time
where the time goes in v8:
time: 104 us; the launch traced here: 103 us
  Pallas kernels  103 us (99%)
    pallas_call x1, Pallas kernels, per_device(): pl.pallas_call(layer_kernel, out_shape=pltpu.VMEM((tokens, columns), bf16...  103 us

profile of v8, /device:TPU:8, one launch (start us, length us, event | category | flops | bytes accessed | tf_op | source)
XLA Modules:
  0.0 103.5 jit_solution(1507282649770640861)
XLA Ops:
  0.0 102.6 %layer.1 = bf16[256,448]{1,0:T(8,128)(2,1)S(1)} custom-call(bf16[256,1536]{1,0:T(8,128)(2,1)} %ql_in.1, bf16[576,256]{1,0:T(8,128)(2,1)} %bitcast.5, bf16[96,1536]{1,0:T(8,128)(2,1)} %qw_in.1, bf16[32,2048]{1,0:T(8,128)(2,1)} %kvw_in.1, bf16[448,1024]{1,0:T(8,128)(2,1)} %bitcast.4, f32[1,512]{1,0:T(1,128)} %bitcast.7, s32[1,4096]{1,0:T(1,128)} %bitcast.6, ...), custom_call_target="tpu_custom_call" | custom-call | tf_op jit(solution)/shard_map/layer/pallas_call | solution.py:652
  102.7 0.8 copy.9
